TPU v7x, 32 devices: a whole 2x2x4 slice. The times are simulated.
32 devices in a mesh: tok: 16 (over z, x, core), ffn: 2 (over y).
Axes of the slice: x: 2, y: 2, z: 4, core: 2. Of those that a mesh axis runs over, the one named last changes fastest.
Arguments:
- tokens: bfloat16 [16384, 768], P(('tok', 'ffn')), may hold values from -6 to 6
- rel_ids: int32 [32, 512, 512], P(('tok', 'ffn')), may hold values from 1 to 511, as said below
- mask_pos: int32 [32, 80], P(('tok', 'ffn')), may hold values from -1 to 511, as said below
- grad_vals: bfloat16 [32, 80, 768], P(('tok', 'ffn')), may hold values from -6 to 6
- w_query: bfloat16 [768, 768], replicated, may hold values from -0.21875 to 0.21875
- w_key: bfloat16 [768, 768], replicated, may hold values from -0.21875 to 0.21875
- w_value: bfloat16 [768, 768], replicated, may hold values from -0.21875 to 0.21875
- w_out: bfloat16 [768, 768], replicated, may hold values from -3 to 3
- b_query: float32 [768], replicated, may hold values from -3 to 3
- b_key: float32 [768], replicated, may hold values from -3 to 3
- b_value: float32 [768], replicated, may hold values from -3 to 3
- b_out: float32 [768], replicated, may hold values from -3 to 3
- rel_table: bfloat16 [512, 768], replicated, may hold values from -6 to 6
- ln1_gain: float32 [768], replicated, may hold values from 0.5 to 1.5
- ln1_bias: float32 [768], replicated, may hold values from -2 to 2
- w_in: bfloat16 [768, 3072], P(None, 'ffn'), may hold values from -0.21875 to 0.21875
- b_in: float32 [3072], P('ffn'), may hold values from -3 to 3
- w_down: bfloat16 [3072, 768], P('ffn'), may hold values from -0.109375 to 0.109375
- b_down: float32 [768], replicated, may hold values from -2 to 2
- ln2_gain: float32 [768], replicated, may hold values from 0.5 to 1.5
- ln2_bias: float32 [768], replicated, may hold values from -2 to 2
Outputs:
- output: bfloat16 [16384, 768], P(('tok', 'ffn'))
- grad_tokens: float32 [16384, 768], P(('tok', 'ffn'))
- grad_w_query: float32 [768, 768], P(('tok', 'ffn'))
- grad_w_key: float32 [768, 768], P(('tok', 'ffn'))
- grad_w_value: float32 [768, 768], P(('tok', 'ffn'))
- grad_w_out: float32 [768, 768], P(('tok', 'ffn'))
- grad_b_query: float32 [768], P(('tok', 'ffn'))
- grad_b_key: float32 [768], P(('tok', 'ffn'))
- grad_b_value: float32 [768], P(('tok', 'ffn'))
- grad_b_out: float32 [768], P(('tok', 'ffn'))
- grad_rel_table: float32 [512, 768], P(('tok', 'ffn'))
- grad_ln1_gain: float32 [768], P(('tok', 'ffn'))
- grad_ln1_bias: float32 [768], P(('tok', 'ffn'))
- grad_w_in: float32 [768, 3072], P('tok', 'ffn')
- grad_b_in: float32 [2, 1536], P('ffn', 'tok')
- grad_w_down: float32 [3072, 768], P('ffn', 'tok')
- grad_b_down: float32 [768], P(('tok', 'ffn'))
- grad_ln2_gain: float32 [768], P(('tok', 'ffn'))
- grad_ln2_bias: float32 [768], P(('tok', 'ffn'))
Inputs may be any that keep to these rules, and one draw needn't show every extreme that they name: `mask_pos`: row s names distinct positions of sequence s in its first slots and -1 in the others; each row names 64 to 80 positions, and some row names 80. rel_ids[s, i, j] = 256 + the DeBERTa log bucket (identity up to 128, logarithmic beyond, maximum position 512) of p_i - p_j, where p_i counts word starts before token i of sequence s, tokens of one word sharing it; so rel_ids[s, j, i] = 512 - rel_ids[s, i, j].
All inputs are finite; a program needn't handle non-finite values.
Results may differ from a plain program's by a relative error of at most 0.034.
Values may be sent and summed in bfloat16 or wider, within the bound.
No kernel may reach another device: no remote copies, remote signals or barrier semaphores. Data moves between devices by JAX's collectives and lax.ppermute only.
A program may use at most 256 MiB of HBM per device.

v0:
```python
import functools
import math

import numpy as np

import jax
import jax.numpy as jnp
from jax import lax
from jax.experimental import pallas as pl
from jax.experimental.pallas import tpu as pltpu
from jax.sharding import PartitionSpec as P

HEAD = 64
LANES = 128
HALF = 64
ROWS = 32
norm_eps = 1e-07
bf16 = jnp.bfloat16
f32 = jnp.float32


def dot_nn(first_op, second_op):
    return lax.dot_general(
        first_op, second_op, (((1,), (0,)), ((), ())), preferred_element_type=f32
    )


def dot_nt(first_op, second_op):
    return lax.dot_general(
        first_op, second_op, (((1,), (1,)), ((), ())), preferred_element_type=f32
    )


def dot_tn(first_op, second_op):
    return lax.dot_general(
        first_op, second_op, (((0,), (0,)), ((), ())), preferred_element_type=f32
    )


def distance_rows(seq_len, table_rows):
    side = table_rows // 2
    middle = side // 2
    rows = []
    for m in range(2 * seq_len):
        offset = max(seq_len - 1 - m, 1 - seq_len)
        size = abs(offset)
        if size > middle:
            ratio = math.log(size / middle) / math.log((2 * side - 1) / middle)
            size = int(math.ceil(ratio * (middle - 1))) + middle
        rows.append(side + (size if offset > 0 else -size))
    return np.array(rows, dtype=np.int32)


def lane_iota(rows=1):
    return lax.broadcasted_iota(jnp.int32, (rows, LANES), 1)


def member_chunk(words, c):
    return (words == lane_iota(words.shape[0]) + c * LANES).astype(f32).astype(bf16)


def id_bases(rel_ref, base):
    seq = rel_ref.shape[0]
    chunks = seq // LANES
    last = chunks * 2 - 2
    for g in range(seq // HALF):
        for c in range(chunks):
            block = rel_ref[g * HALF : (g + 1) * HALF, c * LANES : (c + 1) * LANES]
            base[g * chunks + c] = jnp.minimum(jnp.min(block) // HALF, last)


def both_alignments(table):
    return jnp.concatenate([table, table[HALF:], table[:HALF]], axis=0)


def longest(rows):
    wide = rows.astype(f32)
    return jnp.sqrt(jnp.max(jnp.sum(wide * wide, axis=1, keepdims=True)))


def pack_heads(first, second, dest, top):
    top = jnp.maximum(top, 1e-30)
    scale = 32000.0 / top
    upper = (first * scale).astype(jnp.int32)
    lower = (second * scale).astype(jnp.int32)
    dest[...] = upper * 65536 + lower
    return top * (1.0 / 32000.0)


def unpack_heads(words, step):
    lower = lax.shift_right_arithmetic(lax.shift_left(words, 16), 16)
    return words.astype(f32) * (step * (1.0 / 65536.0)), lower.astype(f32) * step


def picked_words(source, rel_ref, base, rows, c):
    chunks = rel_ref.shape[1] // LANES
    first = base[(rows.start // HALF) * chunks + c]
    place = rel_ref[rows, c * LANES : (c + 1) * LANES] - first * HALF
    index = place & (LANES - 1)
    at = pl.multiple_of((first % 2) * (chunks * LANES) + (first // 2) * LANES, LANES)
    near = jnp.take_along_axis(source[rows, pl.ds(at, LANES)], index, axis=1)
    at = pl.multiple_of(at + LANES, LANES)
    far = jnp.take_along_axis(source[rows, pl.ds(at, LANES)], index, axis=1)
    return jnp.where(place < LANES, near, far)


def unshift_in_order(source, words_ref, base, dest):
    seq = words_ref.shape[0]
    chunks = seq // LANES
    lane = lane_iota()
    zero = jnp.zeros((ROWS, LANES), f32)
    for g in range(chunks):
        first = base[g]
        for sub in range(LANES // ROWS):
            start = g * LANES + sub * ROWS
            rows = slice(start, start + ROWS)
            place = lane - (seq - 1) + words_ref[rows, :] + first * LANES
            index = place & (LANES - 1)
            turned = [
                jnp.take_along_axis(
                    source[rows, c * LANES : (c + 1) * LANES], index, axis=1
                )
                for c in range(chunks)
            ]

            def pick(c):
                return turned[c] if 0 <= c < chunks else zero

            near = place >= 0
            mid = place >= -LANES
            for c in range(chunks + 2):
                value = jnp.where(near, pick(c), jnp.where(mid, pick(c - 1), pick(c - 2)))
                at = pl.multiple_of((first + c) * LANES, LANES)
                dest[rows, pl.ds(at, LANES)] = value.astype(bf16)


def group_bases(words, base):
    seq = words.shape[0]
    for g in range(seq // LANES):
        top = jnp.max(words[g * LANES : (g + 1) * LANES])
        base[g] = (seq - 1 - top) // LANES


def softmax_weights(scores):
    factor = math.log2(math.e) / math.sqrt(3.0 * HEAD)
    top = jnp.max(functools.reduce(jnp.maximum, scores), axis=1, keepdims=True)
    return [jnp.exp2((score - top) * factor) for score in scores]


def head_lanes(a):
    return (lane_iota() < HEAD) if a == 0 else (lane_iota() >= HEAD)


def row_of(ref):
    return ref[...].reshape(1, ref.shape[0])


def norm_stats(values):
    centered = values - jnp.mean(values, axis=1, keepdims=True)
    inv_std = lax.rsqrt(jnp.mean(centered * centered, axis=1, keepdims=True) + norm_eps)
    return centered * inv_std, inv_std


def norm_backward(upstream, normed, inv_std, norm_gain):
    scaled = upstream * norm_gain
    adjusted = (
        scaled
        - jnp.mean(scaled, axis=1, keepdims=True)
        - normed * jnp.mean(scaled * normed, axis=1, keepdims=True)
    )
    return inv_std * adjusted, col_sum(upstream * normed), col_sum(upstream)


def col_sum(values):
    return jnp.sum(values, axis=0, keepdims=True)


def normal_cdf(pre_act):
    return 0.5 * (1.0 + lax.erf(pre_act * (1.0 / math.sqrt(2.0))))


def picked_kernel(
    pos_ref, rel_ref, qc_ref, k_ref, v_ref, pk_ref, pq_ref,
    x_ref, wo_ref, bo_ref, gain_ref, bias_ref,
    ctx_ref, prob_ref, key_ref, word_ref, wordc_ref, normed_ref, inv_ref, low_ref,
    packed, cpick, relc, keyc, attn, base,
):
    seq = k_ref.shape[0]
    picks = qc_ref.shape[0]
    chunks = seq // LANES

    @pl.when(pl.program_id(0) == 0)
    def _():
        row = lax.broadcasted_iota(jnp.int32, (seq, seq), 0)
        col = lax.broadcasted_iota(jnp.int32, (seq, seq), 1)
        side = pk_ref.shape[0] // 2
        step = jnp.sum(jnp.where(col == row - 1, rel_ref[...] - side, 0), axis=1, keepdims=True)
        steps = jnp.broadcast_to(step.astype(f32), (seq, LANES)).astype(bf16)
        word_ref[...] = dot_nn((col <= row).astype(f32).astype(bf16), steps).astype(jnp.int32)
        id_bases(rel_ref, base)
        for n in range(picks):
            place = jnp.maximum(pos_ref[n], 0)
            relc[n : n + 1, :] = rel_ref[pl.ds(place, 1), :]
            wordc_ref[n : n + 1, :] = word_ref[pl.ds(place, 1), :]

    zero = jnp.zeros((), bf16)
    table = both_alignments(pq_ref[...])
    keys = [dot_nt(jnp.where(head_lanes(a), k_ref[...], zero), table) for a in range(2)]
    unit = pack_heads(keys[0], keys[1], packed, longest(k_ref[...]) * longest(pq_ref[...]))
    for a in range(2):
        cpick[a] = dot_nt(jnp.where(head_lanes(a), qc_ref[...], zero), pk_ref[...])
    for g in range(chunks):
        for c in range(chunks):
            parts = []
            for start in range(g * LANES, (g + 1) * LANES, ROWS):
                parts.append(picked_words(packed, rel_ref, base, slice(start, start + ROWS), c))
            block = jnp.concatenate(parts, axis=0).T
            for a, value in enumerate(unpack_heads(block, unit)):
                key_ref[a, c * LANES : (c + 1) * LANES, g * LANES : (g + 1) * LANES] = value

    for n in range(picks):
        place = jnp.maximum(pos_ref[n], 0)
        for a in range(2):
            keyc[a, n : n + 1, :] = key_ref[a, pl.ds(place, 1), :]
    for a in range(2):
        mine = head_lanes(a)
        direct = dot_nt(jnp.where(mine, qc_ref[...], zero), k_ref[...])
        scores = []
        for c in range(chunks):
            ids = relc[:, c * LANES : (c + 1) * LANES]
            index = ids & (LANES - 1)
            value = jnp.take_along_axis(cpick[a, :, :LANES], index, axis=1)
            for n in range(1, pk_ref.shape[0] // LANES):
                other = cpick[a, :, n * LANES : (n + 1) * LANES]
                value = jnp.where(
                    ids >= n * LANES, jnp.take_along_axis(other, index, axis=1), value
                )
            cols = slice(c * LANES, (c + 1) * LANES)
            scores.append(direct[:, cols] + value + keyc[a, :, cols])
        weights = softmax_weights(scores)
        inverse = 1.0 / jnp.sum(sum(weights[1:], weights[0]), axis=1, keepdims=True)
        probs = jnp.concatenate([(weight * inverse).astype(bf16) for weight in weights], axis=1)
        prob_ref[a] = probs
        mixed = dot_nn(probs, v_ref[...]).astype(bf16)
        ctx_ref[...] = mixed if a == 0 else jnp.where(mine, mixed, ctx_ref[...])

    part = dot_nn(ctx_ref[...], wo_ref[...])

    @pl.when(pl.program_id(0) == 0)
    def _():
        attn[...] = x_ref[...].astype(f32) + row_of(bo_ref) + part

    @pl.when(pl.program_id(0) > 0)
    def _():
        attn[...] += part

    @pl.when(pl.program_id(0) == pl.num_programs(0) - 1)
    def _():
        normed, inv_std = norm_stats(attn[...])
        normed_ref[...] = normed
        inv_ref[...] = jnp.broadcast_to(inv_std, (picks, LANES))
        low_ref[...] = (normed * row_of(gain_ref) + row_of(bias_ref)).astype(bf16)


def attend_picked(
    positions, rel_ids, q_pick, k, v, pos_query, pos_key, x_pick, w_out, b_out, gain, bias
):
    seq, width = k.shape
    picks = q_pick.shape[0]
    table = pos_key.shape[0]
    pairs = width // LANES
    whole = lambda rows, cols: pl.BlockSpec((rows, cols), lambda h: (0, 0))
    line = pl.BlockSpec((width,), lambda h: (0,))
    col = lambda rows: pl.BlockSpec((rows, LANES), lambda h: (0, h))
    heads = lambda rows: pl.BlockSpec((2, rows, seq), lambda h: (h, 0, 0))
    return pl.pallas_call(
        picked_kernel,
        grid=(pairs,),
        in_specs=[
            pl.BlockSpec(memory_space=pltpu.SMEM), whole(seq, seq),
            col(picks), col(seq), col(seq), col(table), col(table),
            whole(picks, width), pl.BlockSpec((LANES, width), lambda h: (h, 0)), line, line, line,
        ],
        out_specs=[
            col(picks), heads(picks), heads(seq), whole(seq, LANES), whole(picks, LANES),
            whole(picks, width), whole(picks, LANES), whole(picks, width),
        ],
        out_shape=[
            jax.ShapeDtypeStruct((picks, width), bf16),
            jax.ShapeDtypeStruct((2 * pairs, picks, seq), bf16),
            jax.ShapeDtypeStruct((2 * pairs, seq, seq), f32),
            jax.ShapeDtypeStruct((seq, LANES), jnp.int32),
            jax.ShapeDtypeStruct((picks, LANES), jnp.int32),
            jax.ShapeDtypeStruct((picks, width), f32),
            jax.ShapeDtypeStruct((picks, LANES), f32),
            jax.ShapeDtypeStruct((picks, width), bf16),
        ],
        scratch_shapes=[
            pltpu.VMEM((seq, 2 * table), jnp.int32),
            pltpu.VMEM((2, picks, table), f32),
            pltpu.VMEM((picks, seq), jnp.int32),
            pltpu.VMEM((2, picks, seq), f32),
            pltpu.VMEM((picks, width), f32),
            pltpu.SMEM((seq // HALF * (seq // LANES),), jnp.int32),
        ],
        compiler_params=pltpu.CompilerParams(vmem_limit_bytes=48 * 2**20),
        name="attend_picked",
    )(
        positions, rel_ids, q_pick, k, v, pos_key, pos_query, x_pick, w_out, b_out, gain, bias
    )


def full_kernel(rel_ref, q_ref, k_ref, v_ref, pk_ref, key_ref, ctx_ref, packed, direct, low, base):
    seq = q_ref.shape[0]
    chunks = seq // LANES

    @pl.when(pl.program_id(0) == 0)
    def _():
        id_bases(rel_ref, base)

    zero = jnp.zeros((), bf16)
    table = both_alignments(pk_ref[...])
    far = []
    for a in range(2):
        q_a = jnp.where(head_lanes(a), q_ref[...], zero)
        far.append(dot_nt(q_a, table))
        direct[a] = dot_nt(q_a, k_ref[...])
    unit = pack_heads(far[0], far[1], packed, longest(q_ref[...]) * longest(pk_ref[...]))
    for start in range(0, seq, HALF):
        rows = slice(start, start + HALF)
        scores = [[], []]
        for c in range(chunks):
            cols = slice(c * LANES, (c + 1) * LANES)
            values = unpack_heads(picked_words(packed, rel_ref, base, rows, c), unit)
            for a in range(2):
                scores[a].append(values[a] + direct[a, rows, cols] + key_ref[a, rows, cols])
        for a in range(2):
            for c, weight in enumerate(softmax_weights(scores[a])):
                low[a, rows, c * LANES : (c + 1) * LANES] = weight.astype(bf16)
    mixed = [
        dot_nn(low[a], jnp.where(head_lanes(a), v_ref[...], jnp.ones((), bf16))) for a in range(2)
    ]
    upper = head_lanes(0)
    totals = pltpu.roll(jnp.where(upper, mixed[1], mixed[0]), HEAD, 1)
    ctx_ref[...] = (jnp.where(upper, mixed[0], mixed[1]) * (1.0 / totals)).astype(bf16)


def attend_full(rel_ids, q, k, v, pos_key, key_scores, first, pairs):
    seq = k.shape[0]
    table = pos_key.shape[0]
    col = lambda rows: pl.BlockSpec((rows, LANES), lambda h: (0, h + first))
    return pl.pallas_call(
        full_kernel,
        grid=(pairs,),
        in_specs=[
            pl.BlockSpec((seq, seq), lambda h: (0, 0)),
            col(seq), col(seq), col(seq), col(table),
            pl.BlockSpec((2, seq, seq), lambda h: (h + first, 0, 0)),
        ],
        out_specs=pl.BlockSpec((seq, LANES), lambda h: (0, h)),
        out_shape=jax.ShapeDtypeStruct((seq, pairs * LANES), bf16),
        scratch_shapes=[
            pltpu.VMEM((seq, 2 * table), jnp.int32),
            pltpu.VMEM((2, seq, seq), f32),
            pltpu.VMEM((2, seq, seq), bf16),
            pltpu.SMEM((seq // HALF * (seq // LANES),), jnp.int32),
        ],
        compiler_params=pltpu.CompilerParams(vmem_limit_bytes=48 * 2**20),
        name="attend_full",
    )(rel_ids, q, k, v, pos_key, key_scores)


def back_kernel(
    me_ref, row_ref, order_ref, word_ref, wordc_ref, qc_ref, k_ref, v_ref, prob_ref, pk_ref, pq_ref,
    dz2_ref, mine_ref, got_ref, normed_ref, inv_ref, gain_ref, wo_ref, early_ref,
    dq_ref, dk_ref, dv_ref, dpos_ref, dz1_ref, dattn_ref, sum_ref,
    side, sidec, moved, movedc, grel, expand, turned_expand, base,
):
    seq = k_ref.shape[0]
    picks = qc_ref.shape[0]
    table = pk_ref.shape[0]
    chunks = seq // LANES

    @pl.when(pl.program_id(0) == 0)
    def _():
        words = word_ref[...]
        for c in range(chunks):
            side[:, c * LANES : (c + 1) * LANES] = member_chunk(words, c)
            sidec[:, c * LANES : (c + 1) * LANES] = member_chunk(wordc_ref[...], c)
        group_bases(words, base)
        moved[...] = jnp.zeros_like(moved)
        for c in range(table // LANES):
            cols = slice(c * LANES, (c + 1) * LANES)
            expand[:, cols] = member_chunk(row_ref[...], c)
            source = block_source(order_ref, me_ref, cols, table)
            turned_expand[:, cols] = (row_ref[...] == source).astype(f32).astype(bf16)
        dh1 = dz2_ref[...] + mine_ref[...].astype(f32) + got_ref[...].astype(f32)
        dz1, g_gain, g_bias = norm_backward(dh1, normed_ref[...], inv_ref[:, :1], row_of(gain_ref))
        dz1_ref[...] = dz1
        dattn = dz1.astype(bf16)
        dattn_ref[...] = dattn
        sum_ref[...] = jnp.concatenate(
            [col_sum(dattn.astype(f32)), g_gain, g_bias, early_ref[:5]], axis=0
        )

    lane = lane_iota()
    scale = 1.0 / math.sqrt(3.0 * HEAD)
    zero = jnp.zeros((), bf16)
    far_key = dot_nn(expand[...], pk_ref[...]).astype(bf16)
    far_query = dot_nn(expand[...], pq_ref[...]).astype(bf16)
    dctx = dot_nt(dattn_ref[...], wo_ref[...]).astype(bf16)
    for a in range(2):
        mine = head_lanes(a)
        keep = lambda value: jnp.where(mine, value, zero)
        dctx_a = keep(dctx)
        q_a = keep(qc_ref[...])
        k_a = keep(k_ref[...])
        side[:, seq:] = k_a
        sidec[:, seq:] = q_a
        dprobs = dot_nt(dctx_a, v_ref[...])
        probs = prob_ref[a].astype(f32)
        prod = probs * dprobs
        gs = ((prod - probs * jnp.sum(prod, axis=1, keepdims=True)) * scale).astype(bf16)
        dv = dot_tn(prob_ref[a], dctx_a)

        out = dot_nn(gs, side[...])
        place = lane - (seq - 1) + wordc_ref[...]
        index = place & (LANES - 1)
        turned = [
            jnp.take_along_axis(out[:, c * LANES : (c + 1) * LANES], index, axis=1)
            for c in range(chunks)
        ]
        blank = jnp.zeros((picks, LANES), f32)
        for c in range(2 * chunks):
            value = turned[c] if c < chunks else blank
            for n in range(1, chunks + 1):
                other = turned[c - n] if 0 <= c - n < chunks else blank
                value = jnp.where(place < -LANES * (n - 1), other, value)
            movedc[:, c * LANES : (c + 1) * LANES] = value.astype(bf16)
        dq = out[:, seq:] + dot_nn(movedc[...], keep(far_key))
        dpk = dot_tn(movedc[...], q_a)

        out = dot_tn(gs, sidec[...])
        grel[...] = out[:, :seq]
        unshift_in_order(grel, word_ref, base, moved)
        dk = out[:, seq:] + dot_nn(moved[:, : 2 * seq], keep(far_query))
        dpq = dot_tn(moved[:, : 2 * seq], k_a)
        dpk = dot_tn(turned_expand[...], dpk.astype(bf16))
        dpq = dot_tn(turned_expand[...], dpq.astype(bf16))
        for ref, value in (
            (dq_ref, dq), (dk_ref, dk), (dv_ref, dv), (dpos_ref.at[0], dpk), (dpos_ref.at[1], dpq),
        ):
            low = value.astype(bf16)
            ref[...] = low if a == 0 else jnp.where(mine, low, ref[...])


def attend_back(
    me, table_of, order, words, words_pick, q_pick, k, v, probs, pos_query, pos_key,
    dz2, mine, got, normed, inv_std, gain, w_out, early,
):
    seq, width = k.shape
    picks = q_pick.shape[0]
    table = pos_key.shape[0]
    pairs = width // LANES
    whole = lambda value: pl.BlockSpec(value.shape, lambda h: (0,) * value.ndim)
    col = lambda rows: pl.BlockSpec((rows, LANES), lambda h: (0, h))
    shape = lambda rows: jax.ShapeDtypeStruct((rows, width), bf16)
    return pl.pallas_call(
        back_kernel,
        grid=(pairs,),
        in_specs=[
            pl.BlockSpec(memory_space=pltpu.SMEM),
            whole(table_of), whole(order), whole(words), whole(words_pick),
            col(picks), col(seq), col(seq),
            pl.BlockSpec((2, picks, seq), lambda h: (h, 0, 0)),
            col(table), col(table),
            whole(dz2), whole(mine), whole(got), whole(normed), whole(inv_std), whole(gain),
            pl.BlockSpec((LANES, width), lambda h: (h, 0)), whole(early),
        ],
        out_specs=[
            col(picks), col(seq), col(seq),
            pl.BlockSpec((2, table, LANES), lambda h: (0, 0, h)),
            whole(dz2), whole(dz2), whole(early),
        ],
        out_shape=[
            shape(picks), shape(seq), shape(seq),
            jax.ShapeDtypeStruct((2, table, width), bf16),
            jax.ShapeDtypeStruct((picks, width), f32),
            shape(picks),
            jax.ShapeDtypeStruct(early.shape, f32),
        ],
        scratch_shapes=[
            pltpu.VMEM((seq, seq + LANES), bf16),
            pltpu.VMEM((picks, seq + LANES), bf16),
            pltpu.VMEM((seq, 2 * seq + LANES), bf16),
            pltpu.VMEM((picks, 2 * seq), bf16),
            pltpu.VMEM((seq, seq), f32),
            pltpu.VMEM((2 * seq, table), bf16),
            pltpu.VMEM((2 * seq, table), bf16),
            pltpu.SMEM((seq // LANES,), jnp.int32),
        ],
        compiler_params=pltpu.CompilerParams(vmem_limit_bytes=48 * 2**20),
        name="attend_back",
    )(
        me, table_of, order, words, words_pick, q_pick, k, v, probs, pos_key, pos_query,
        dz2, mine, got, normed, inv_std, gain, w_out, early,
    )


def block_source(order_ref, me_ref, cols, length):
    relative = jnp.where(me_ref[1] == 0, order_ref[0:1, cols], order_ref[1:2, cols])
    return (me_ref[0] ^ relative) * (length // me_ref[2]) + order_ref[2:3, cols]


def turn_kernel(
    me_ref, order_ref, relorder_ref, x_ref, xpick_ref, cpick_ref, rel_ref,
    x_out, xpick_out, cpick_out, rel_out, rows,
):
    width, group = x_ref.shape[1], x_out.shape[1]
    table = rel_ref.shape[0]

    @pl.when(pl.program_id(0) == 0)
    def _():
        source = block_source(relorder_ref, me_ref, slice(None), table)
        spot = lax.broadcasted_iota(jnp.int32, (table, table), 0)
        rows[...] = dot_tn((spot == source).astype(f32).astype(bf16), rel_ref[...]).astype(bf16)

    source = block_source(order_ref, me_ref, slice(None), width)
    spot = lax.broadcasted_iota(jnp.int32, (width, group), 0)
    chosen = (spot == source).astype(f32).astype(bf16)
    for ref, out in ((x_ref, x_out), (xpick_ref, xpick_out), (cpick_ref, cpick_out), (rows, rel_out)):
        out[...] = dot_nn(ref[...], chosen).astype(bf16)


def turn_blocks(me, order, rel_order, x, x_pick, ctx_pick, rel_table):
    width = x.shape[1]
    group = 2 * LANES
    whole = lambda value: pl.BlockSpec(value.shape, lambda n: (0, 0))
    col = lambda value: pl.BlockSpec((value.shape[0], group), lambda n: (0, n))
    given = [x, x_pick, ctx_pick, rel_table]
    return pl.pallas_call(
        turn_kernel,
        grid=(width // group,),
        in_specs=[pl.BlockSpec(memory_space=pltpu.SMEM), col(order), whole(rel_order)]
        + [whole(value) for value in given],
        out_specs=[col(value) for value in given],
        out_shape=[jax.ShapeDtypeStruct(value.shape, bf16) for value in given],
        scratch_shapes=[pltpu.VMEM(rel_table.shape, bf16)],
        compiler_params=pltpu.CompilerParams(vmem_limit_bytes=48 * 2**20),
        name="turn_blocks",
    )(me, order, rel_order, *given)


def ffn_picked_kernel(
    mine_ref, their_ref, win_ref, bin_ref, down_ref, part_ref, theirs_ref, hidden_ref, slope_ref, total
):
    step = pl.program_id(0)
    rows = jnp.concatenate([mine_ref[...], their_ref[...]], axis=0)
    pre = dot_nn(rows, win_ref[...]) + row_of(bin_ref)
    cdf = normal_cdf(pre)
    hidden = (pre * cdf).astype(bf16)
    hidden_ref[...] = hidden
    slope_ref[...] = cdf + pre * (jnp.exp(-0.5 * pre * pre) * (1.0 / math.sqrt(2.0 * math.pi)))
    part = dot_nn(hidden, down_ref[...])
    total[...] = jnp.where(step == 0, part, total[...] + part)

    @pl.when(step == pl.num_programs(0) - 1)
    def _():
        count = mine_ref.shape[0]
        part_ref[...] = total[:count].astype(bf16)
        theirs_ref[...] = total[count:].astype(bf16)


def ffn_picked(mine, theirs, w_in, b_in, w_down):
    picks, width = mine.shape
    hidden_cols = w_in.shape[1]
    tile = hidden_cols // 3
    whole = pl.BlockSpec((picks, width), lambda n: (0, 0))
    col = lambda rows: pl.BlockSpec((rows, tile), lambda n: (0, n))
    return pl.pallas_call(
        ffn_picked_kernel,
        grid=(3,),
        in_specs=[
            whole, whole, col(width), pl.BlockSpec((tile,), lambda n: (n,)),
            pl.BlockSpec((tile, width), lambda n: (n, 0)),
        ],
        out_specs=[whole, whole, col(2 * picks), col(2 * picks)],
        out_shape=[
            jax.ShapeDtypeStruct((picks, width), bf16),
            jax.ShapeDtypeStruct((picks, width), bf16),
            jax.ShapeDtypeStruct((2 * picks, hidden_cols), bf16),
            jax.ShapeDtypeStruct((2 * picks, hidden_cols), f32),
        ],
        scratch_shapes=[pltpu.VMEM((2 * picks, width), f32)],
        compiler_params=pltpu.CompilerParams(vmem_limit_bytes=48 * 2**20),
        name="ffn_picked",
    )(mine, theirs, w_in, b_in, w_down)


def norm_picked_kernel(
    normed_ref, gain1_ref, bias1_ref, mine_ref, got_ref, bdown_ref, gain2_ref, grad_ref, pick_ref,
    dz2_ref, low_ref, sum_ref,
):
    h1 = normed_ref[...] * row_of(gain1_ref) + row_of(bias1_ref)
    branch = mine_ref[...].astype(f32) + got_ref[...].astype(f32) + row_of(bdown_ref)
    normed, inv_std = norm_stats(h1 + branch)
    used = jnp.sum(pick_ref[...].astype(f32), axis=1, keepdims=True)
    cot = jnp.where(used > 0.0, grad_ref[...].astype(f32), 0.0)
    dz2, g_gain, g_bias = norm_backward(cot, normed, inv_std, row_of(gain2_ref))
    dz2_ref[...] = dz2
    low = dz2.astype(bf16)
    low_ref[...] = low
    sum_ref[...] = jnp.concatenate(
        [col_sum(low.astype(f32)), g_gain, g_bias, jnp.zeros((5, h1.shape[1]), f32)], axis=0
    )


def norm_picked(normed, gain1, bias1, mine, got, b_down, gain2, grads, pick):
    picks, width = normed.shape
    return pl.pallas_call(
        norm_picked_kernel,
        out_shape=[
            jax.ShapeDtypeStruct((picks, width), f32),
            jax.ShapeDtypeStruct((picks, width), bf16),
            jax.ShapeDtypeStruct((8, width), f32),
        ],
        name="norm_picked",
    )(normed, gain1, bias1, mine, got, b_down, gain2, grads, pick)


def ffn_back_kernel(
    mine_ref, their_ref, win_ref, down_ref, slope_ref, part_ref, theirs_ref, dpre_ref, sum_ref, total
):
    step = pl.program_id(0)
    rows = jnp.concatenate([mine_ref[...], their_ref[...]], axis=0)
    dpre = (dot_nt(rows, down_ref[...]) * slope_ref[...]).astype(bf16)
    dpre_ref[...] = dpre
    sum_ref[...] = jnp.broadcast_to(col_sum(dpre.astype(f32)), sum_ref.shape)
    part = dot_nt(dpre, win_ref[...])
    total[...] = jnp.where(step == 0, part, total[...] + part)

    @pl.when(step == pl.num_programs(0) - 1)
    def _():
        count = mine_ref.shape[0]
        part_ref[...] = total[:count].astype(bf16)
        theirs_ref[...] = total[count:].astype(bf16)


def ffn_back(mine, theirs, w_in, w_down, slope):
    picks, width = mine.shape
    hidden_cols = w_in.shape[1]
    tile = hidden_cols // 3
    whole = pl.BlockSpec((picks, width), lambda n: (0, 0))
    col = lambda rows: pl.BlockSpec((rows, tile), lambda n: (0, n))
    return pl.pallas_call(
        ffn_back_kernel,
        grid=(3,),
        in_specs=[
            whole, whole, col(width), pl.BlockSpec((tile, width), lambda n: (n, 0)), col(2 * picks)
        ],
        out_specs=[whole, whole, col(2 * picks), col(8)],
        out_shape=[
            jax.ShapeDtypeStruct((picks, width), bf16),
            jax.ShapeDtypeStruct((picks, width), bf16),
            jax.ShapeDtypeStruct((2 * picks, hidden_cols), bf16),
            jax.ShapeDtypeStruct((8, hidden_cols), f32),
        ],
        scratch_shapes=[pltpu.VMEM((2 * picks, width), f32)],
        compiler_params=pltpu.CompilerParams(vmem_limit_bytes=48 * 2**20),
        name="ffn_back",
    )(mine, theirs, w_in, w_down, slope)


def ffn_grads_kernel(mine_ref, their_ref, dmine_ref, dtheir_ref, dpre_ref, hidden_ref, out_ref):
    @pl.when(pl.program_id(0) == 0)
    def _():
        rows = jnp.concatenate([mine_ref[...], their_ref[...]], axis=0)
        out_ref[...] = dot_tn(rows, dpre_ref[...]).astype(bf16)

    @pl.when(pl.program_id(0) == 1)
    def _():
        rows = jnp.concatenate([dmine_ref[...], dtheir_ref[...]], axis=0)
        out_ref[...] = dot_tn(rows, hidden_ref[...]).astype(bf16)


def ffn_grads(mine, theirs, dmine, dtheirs, dpre, hidden):
    picks, width = mine.shape
    hidden_cols = dpre.shape[1]
    tile = hidden_cols // 3
    whole = pl.BlockSpec((picks, width), lambda n, t: (0, 0))
    return pl.pallas_call(
        ffn_grads_kernel,
        grid=(2, 3),
        in_specs=[
            whole, whole, whole, whole,
            pl.BlockSpec((2 * picks, tile), lambda n, t: (0, jnp.where(n == 0, t, 2))),
            pl.BlockSpec((2 * picks, tile), lambda n, t: (0, jnp.where(n == 0, 0, t))),
        ],
        out_specs=pl.BlockSpec((width, tile), lambda n, t: (0, 3 * n + t)),
        out_shape=jax.ShapeDtypeStruct((width, 2 * hidden_cols), bf16),
        compiler_params=pltpu.CompilerParams(vmem_limit_bytes=48 * 2**20),
        name="ffn_grads",
    )(mine, theirs, dmine, dtheirs, dpre, hidden)


def ffn_full_kernel(
    x_ref, ctx_ref, ctx2_ref, wo_ref, bo_ref, gain1_ref, bias1_ref,
    win_ref, down_ref, bin_ref, win2_ref, down2_ref, bin2_ref, win3_ref, down3_ref, bin3_ref,
    bdown_ref, gain2_ref, bias2_ref, out_ref, h1, low, total,
):
    step = pl.program_id(0)
    width = x_ref.shape[1]

    @pl.when(step == 0)
    def _():
        attn = dot_nn(ctx_ref[...], wo_ref[: width // 2]) + dot_nn(ctx2_ref[...], wo_ref[width // 2 :])
        normed, _ = norm_stats(x_ref[...].astype(f32) + (attn + row_of(bo_ref)))
        value = normed * row_of(gain1_ref) + row_of(bias1_ref)
        h1[...] = value
        low[...] = value.astype(bf16)
        total[...] = jnp.zeros_like(total)

    def tile(w_ref, d_ref, b_ref):
        pre = dot_nn(low[...], w_ref[...]) + b_ref[...]
        total[...] += dot_nn((pre * normal_cdf(pre)).astype(bf16), d_ref[...])

    @pl.when(step < 4)
    def _():
        tile(win_ref, down_ref, bin_ref)

    @pl.when((step >= 4) & (step < 6))
    def _():
        tile(win2_ref, down2_ref, bin2_ref)

    @pl.when(step >= 6)
    def _():
        tile(win3_ref, down3_ref, bin3_ref)

    @pl.when(step == 7)
    def _():
        normed, _ = norm_stats(h1[...] + (total[...] + row_of(bdown_ref)))
        out_ref[...] = (normed * row_of(gain2_ref) + row_of(bias2_ref)).astype(bf16)


def ffn_full(x, ctx, w_out, b_out, gain1, bias1, shards, b_down, gain2, bias2):
    rows, width = x.shape
    tile = shards[0][0].shape[1] // 4
    whole = lambda value: pl.BlockSpec(value.shape, lambda t: (0,) * value.ndim)
    specs = []
    for first, last in ((0, 4), (4, 6), (6, 8)):
        at = lambda t, first=first, last=last: jnp.clip(t, first, last - 1) - first
        specs += [
            pl.BlockSpec((width, tile), lambda t, at=at: (0, at(t))),
            pl.BlockSpec((tile, width), lambda t, at=at: (at(t), 0)),
            pl.BlockSpec((1, tile), lambda t, at=at: (0, at(t))),
        ]
    head = [x, ctx[0], ctx[1], w_out, b_out, gain1, bias1]
    tail = [b_down, gain2, bias2]
    return pl.pallas_call(
        ffn_full_kernel,
        grid=(8,),
        in_specs=[whole(value) for value in head] + specs + [whole(value) for value in tail],
        out_specs=pl.BlockSpec((rows, width), lambda t: (0, 0)),
        out_shape=jax.ShapeDtypeStruct((rows, width), bf16),
        scratch_shapes=[
            pltpu.VMEM((rows, width), f32), pltpu.VMEM((rows, width), bf16), pltpu.VMEM((rows, width), f32)
        ],
        compiler_params=pltpu.CompilerParams(vmem_limit_bytes=48 * 2**20),
        name="ffn_full",
    )(*head, *[value for shard in shards for value in shard], *tail)


def token_grads_kernel(pick_ref, dz1_ref, dq_ref, dk_ref, dv_ref, wq_ref, wk_ref, wv_ref, out_ref):
    sparse = dz1_ref[...] + dot_nt(dq_ref[...], wq_ref[...])
    upper = sparse.astype(bf16)
    lower = (sparse - upper.astype(f32)).astype(bf16)
    out_ref[...] = (
        dot_nt(dk_ref[...], wk_ref[...])
        + dot_nt(dv_ref[...], wv_ref[...])
        + dot_tn(pick_ref[...], upper)
        + dot_tn(pick_ref[...], lower)
    )


def token_grads(pick, dz1, dq, dk, dv, w_query, w_key, w_value):
    seq, width = dk.shape
    group = 2 * LANES
    whole = lambda value: pl.BlockSpec(value.shape, lambda n: (0, 0))
    col = lambda rows: pl.BlockSpec((rows, group), lambda n: (0, n))
    row = pl.BlockSpec((group, width), lambda n: (n, 0))
    return pl.pallas_call(
        token_grads_kernel,
        grid=(width // group,),
        in_specs=[whole(pick), col(dz1.shape[0]), whole(dq), whole(dk), whole(dv), row, row, row],
        out_specs=col(seq),
        out_shape=jax.ShapeDtypeStruct((seq, width), f32),
        compiler_params=pltpu.CompilerParams(vmem_limit_bytes=48 * 2**20),
        name="token_grads",
    )(pick, dz1, dq, dk, dv, w_query, w_key, w_value)


def grads_kernel(
    half, x_ref, rel_ref, xpick_ref, cpick_ref, dpos_ref,
    dq_ref, dk_ref, dv_ref, dattn_ref, dposk_ref, dposq_ref, wq_ref, wk_ref,
    early_ref, bin_ref, bin2_ref, out_ref, sum_ref,
):
    width = x_ref.shape[1]
    group = 2 * LANES
    seq = x_ref.shape[0]

    def left(ref):
        starts = range(half * LANES, width, group)
        return jnp.concatenate([ref[:, at : at + LANES] for at in starts], axis=1)

    def put(at, value):
        for n in range(value.shape[0] // LANES):
            out_ref[at + n] = value[n * LANES : (n + 1) * LANES].astype(bf16)

    count = width // group
    rel_left = left(rel_ref)
    x_left = left(x_ref)
    put(0, dot_tn(left(xpick_ref), dq_ref[...]) + dot_tn(rel_left, dposq_ref[0]))
    put(count, dot_tn(x_left, dk_ref[...]) + dot_tn(rel_left, dposk_ref[0]))
    put(2 * count, dot_tn(x_left, dv_ref[...]))
    put(3 * count, dot_tn(left(cpick_ref), dattn_ref[...]))
    for n in range(dpos_ref.shape[1] // group):
        rows = slice(n * group + half * LANES, n * group + (half + 1) * LANES)
        put(
            4 * count + n,
            dot_nt(dpos_ref[0, rows, :], wk_ref[...]) + dot_nt(dpos_ref[1, rows, :], wq_ref[...]),
        )
    total = lambda value: col_sum(value.astype(f32))
    sum_ref[...] = jnp.concatenate(
        [
            total(dq_ref[...]) + total(dposq_ref[0]),
            total(dk_ref[...]) + total(dposk_ref[0]),
            total(dv_ref[...]),
            early_ref[:6],
            bin_ref[:1],
            bin2_ref[:1],
            jnp.zeros((5, group), f32),
        ],
        axis=0,
    )


def weight_grads(half, x, rel, x_pick, c_pick, dpos, dq, dk, dv, dattn, w_query, w_key, early, bins):
    seq, width = x.shape
    group = 2 * LANES
    planes = 4 * (width // group) + dpos.shape[1] // group
    whole = lambda value: pl.BlockSpec(value.shape, lambda n: (0,) * value.ndim)
    col = lambda value: pl.BlockSpec((value.shape[0], group), lambda n: (0, n))
    row = lambda value: pl.BlockSpec((group, value.shape[1]), lambda n: (n, 0))
    plane = lambda t: pl.BlockSpec((1, dpos.shape[1], group), lambda n: (t, 0, n))
    return pl.pallas_call(
        functools.partial(grads_kernel, half),
        grid=(width // group,),
        in_specs=[
            whole(x), whole(rel), whole(x_pick), whole(c_pick), whole(dpos),
            col(dq), col(dk), col(dv), col(dattn), plane(0), plane(1), row(w_query), row(w_key),
            col(early), col(bins), pl.BlockSpec((8, group), lambda n: (0, n + width // group)),
        ],
        out_specs=[
            pl.BlockSpec((planes, LANES, group), lambda n: (0, 0, n)),
            pl.BlockSpec((16, group), lambda n: (0, n)),
        ],
        out_shape=[
            jax.ShapeDtypeStruct((planes, LANES, width), bf16),
            jax.ShapeDtypeStruct((16, width), f32),
        ],
        compiler_params=pltpu.CompilerParams(vmem_limit_bytes=48 * 2**20),
        name="weight_grads",
    )(
        x, rel, x_pick, c_pick, dpos, dq, dk, dv, dattn, dpos, dpos, w_query, w_key, early, bins, bins
    )


def swap(values, axis, bit):
    size = lax.axis_size(axis)
    return lax.ppermute(values, axis, [(n, n ^ bit) for n in range(size)])


def after(values, *others):
    return lax.optimization_barrier((values, others))[0]


class Halving:
    def __init__(self, axes, core, near, size):
        rest = [1 << n for n in range(size.bit_length() - 1) if (1 << n) != core]
        near = [bit for bit in near if bit in rest]
        rest = [bit for bit in rest if bit not in near]
        turned = near[-1:] + near[:-1]
        self.axes, self.core, self.size = axes, core, size
        self.orders = [[core] + near + rest, [core] + turned + rest]
        self.steps = len(self.orders[0])
        self.me = lax.axis_index(axes)
        self.upper = (self.me // core) % 2

    def core_of(self, place):
        return (place // self.core) % 2

    def send(self, values, step):
        pairs = [(n, n ^ self.orders[self.core_of(n)][step]) for n in range(self.size)]
        return lax.ppermute(values, self.axes, pairs)

    def bit(self, step):
        first, second = (order[step] for order in self.orders)
        return jnp.where(self.upper == 0, first, second)

    def relative(self, upper):
        masks = []
        for place in range(self.size):
            bits = [(place >> (self.steps - 1 - step)) & 1 for step in range(self.steps)]
            order = self.orders[upper ^ bits[0]]
            mask = 0
            for step, bit in enumerate(bits):
                mask ^= bit * order[step]
            masks.append(mask)
        return np.array(masks, np.int32)

    def order(self, length, unit):
        spots = np.arange(length)
        group = self.size * unit
        place = spots % group // unit
        rows = [self.relative(upper)[place] for upper in range(2)]
        rows.append(spots // group * unit + spots % unit)
        return jnp.asarray(np.stack(rows + [np.zeros_like(spots)] * 5).astype(np.int32))


def local(
    tokens, rel_ids, mask_pos, grad_vals, w_query, w_key, w_value, w_out, b_query, b_key,
    b_value, b_out, rel_table, ln1_gain, ln1_bias, w_in, b_in, w_down, b_down, ln2_gain, ln2_bias,
):
    assert rel_ids.shape[0] == 1
    seq, width = tokens.shape
    table_rows = rel_table.shape[0]
    hidden_cols = w_in.shape[1]
    pairs = width // LANES
    n_tok = lax.axis_size("tok")
    n_ffn = lax.axis_size("ffn")
    n_all = n_tok * n_ffn
    low = lambda value: value.astype(bf16)
    wide = lambda value: value.astype(f32)
    rel_ids, positions, grad_vals = rel_ids[0], mask_pos[0], grad_vals[0]

    over_all = Halving(("tok", "ffn"), n_ffn, [2 * n_ffn, 1, 4 * n_ffn], n_all)
    own, own_rel = width // n_all, table_rows // n_all
    unit = math.gcd(own, own_rel)
    me = jnp.stack([over_all.me, over_all.upper, jnp.int32(n_all)])
    order, rel_order = over_all.order(width, unit), over_all.order(table_rows, unit)
    table_of = jnp.asarray(np.repeat(distance_rows(seq, table_rows)[:, None], LANES, 1))

    core = lax.axis_index("tok") % 2
    half_cols = hidden_cols // 2
    in_half = lax.dynamic_slice_in_dim(w_in, core * half_cols, half_cols, 1)
    bias_row = b_in.reshape(1, hidden_cols)
    bias_half = lax.dynamic_slice_in_dim(bias_row, core * half_cols, half_cols, 1)
    down_half = lax.dynamic_slice_in_dim(w_down, core * half_cols, half_cols, 0)

    pick = low(positions[:, None] == lax.broadcasted_iota(jnp.int32, (positions.shape[0], seq), 1))
    x_pick = low(dot_nn(pick, tokens))
    q_pick = low(dot_nn(x_pick, w_query) + b_query)
    k = low(dot_nn(tokens, w_key) + b_key)
    v = low(dot_nn(tokens, w_value) + b_value)
    pos_query = low(dot_nn(rel_table, w_query) + b_query)
    pos_key = low(dot_nn(rel_table, w_key) + b_key)
    ctx_pick, probs, key_scores, words, words_pick, normed1, inv1, h1_mine = attend_picked(
        positions, rel_ids, q_pick, k, v, pos_query, pos_key, x_pick, w_out, b_out, ln1_gain, ln1_bias
    )

    h1_theirs = swap(h1_mine, "ffn", 1)
    x_turned, x_pick_turned, c_pick_turned, rel_turned = turn_blocks(
        me, order, rel_order, tokens, x_pick, ctx_pick, rel_table
    )
    h1_theirs = after(h1_theirs, x_turned)
    part, theirs, hidden, slope = ffn_picked(h1_mine, h1_theirs, w_in, b_in, w_down)
    got = swap(theirs, "ffn", 1)
    q = low(dot_nn(after(tokens, theirs), w_query) + b_query)
    got = after(got, q)
    dz2, dffn, early = norm_picked(
        normed1, ln1_gain, ln1_bias, part, got, b_down, ln2_gain, grad_vals, pick
    )
    dffn_theirs = swap(dffn, "ffn", 1)
    dpart, dtheirs, dpre, gb_in = ffn_back(dffn, dffn_theirs, w_in, w_down, slope)
    dgot = swap(dtheirs, "ffn", 1)
    gw_ffn = ffn_grads(h1_mine, h1_theirs, dffn, dffn_theirs, after(dpre, dtheirs), hidden)
    dgot = after(dgot, gw_ffn)
    s_ffn = lax.psum_scatter(gw_ffn, "tok", scatter_dimension=0, tiled=True)

    in_half, bias_half, down_half = after((in_half, bias_half, down_half), dgot)
    far_in, far_bias = swap(in_half, "ffn", 1), swap(bias_half, "ffn", 1)
    dq, dk, dv, dpos, dz1, dattn, early = attend_back(
        me, table_of, rel_order, words, words_pick, q_pick, k, v, probs, pos_query, pos_key,
        dz2, dpart, after(dgot, in_half), normed1, inv1, ln1_gain, w_out, early,
    )
    far_in, far_bias = after((far_in, far_bias), dk)

    def grads(half, dk):
        return weight_grads(
            half, x_turned, rel_turned, x_pick_turned, c_pick_turned, dpos, dq, dk, dv, dattn,
            w_query, w_key, early, gb_in,
        )

    all_send, vectors = grads(1, after(dk, far_in))
    near_in, near_bias = swap(far_in, "tok", 1), swap(far_bias, "tok", 1)
    far_down = swap(after(down_half, far_in), "ffn", 1)

    def halves(values, axis):
        size = values.shape[axis] // 2
        cut = lambda at: lax.slice_in_dim(values, at, at + size, axis=axis)
        return cut(0), cut(size)

    add = lambda one, other: low(wide(one) + wide(other))
    all_got = over_all.send(all_send, 0)
    vec_got = over_all.send(vectors, 0)
    all_kept, _ = grads(0, after(dk, all_send))
    all_sums = add(all_kept, after(all_got, all_kept))
    vectors = vectors + vec_got
    shared = lax.broadcasted_iota(jnp.int32, (vectors.shape[0], 1), 0) < 9

    def attend(first, count, q):
        return attend_full(rel_ids, q, k, v, pos_key, key_scores, first, count)

    fills = []
    for step in range(1, over_all.steps):
        kept, sent = halves(all_sums, 1)
        all_got = over_all.send(sent, step)
        vec_got = over_all.send(vectors, step)
        if step == 1:
            fills.append(attend(0, pairs // 2, after(q, sent)))
        elif step == 2:
            fills.append(attend(pairs // 2, pairs - pairs // 2, after(q, sent)))
        elif step == 3:
            fills.append(
                token_grads(pick, dz1, dq, after(dk, sent), dv, w_query, w_key, w_value)
            )
        elif step == 4:
            near_down = swap(far_down, "tok", 1)
            shards = [
                (w_in, w_down, bias_row), (far_in, far_down, far_bias), (near_in, near_down, near_bias)
            ]
            fills.append(
                ffn_full(
                    after(tokens, sent), fills[:2], w_out, b_out, ln1_gain, ln1_bias, shards,
                    b_down, ln2_gain, ln2_bias,
                )
            )
        if step <= 4:
            all_got, vec_got = after((all_got, vec_got), fills[-1])
        all_sums = add(kept, all_got)
        vectors = vectors + jnp.where(shared | (over_all.bit(step) != 1), vec_got, 0.0)
    grad_tokens, output = fills[2:]

    all_sums = all_sums.reshape(all_sums.shape[0] * unit, width)
    s_w = [wide(all_sums[n * own : (n + 1) * own]) for n in range(4)]
    s_rel = wide(all_sums[4 * own :])
    s_vec = lax.dynamic_slice_in_dim(vectors[:9], over_all.me * own, own, 1)
    part = hidden_cols // n_tok
    s_bin = lax.dynamic_slice_in_dim(
        vectors[9 : 9 + hidden_cols // width].reshape(1, hidden_cols), lax.axis_index("tok") * part, part, 1
    )
    return (
        output,
        grad_tokens,
        s_w[0],
        s_w[1],
        s_w[2],
        s_w[3],
        s_vec[0],
        s_vec[1],
        s_vec[2],
        s_vec[3],
        s_rel,
        s_vec[4],
        s_vec[5],
        wide(s_ffn[:, :hidden_cols]),
        s_bin,
        jnp.transpose(wide(s_ffn[:, hidden_cols:])),
        s_vec[6],
        s_vec[7],
        s_vec[8],
    )


def solution(mesh):
    every = ("tok", "ffn")
    placed = (
        P(every, None), P(every, None, None), P(every, None), P(every, None, None),
        P(), P(), P(), P(), P(), P(), P(), P(), P(), P(), P(),
        P(None, "ffn"), P("ffn"), P("ffn", None), P(), P(), P(),
    )
    given = (
        P(every, None), P(every, None),
        P(every, None), P(every, None), P(every, None), P(every, None),
        P(every), P(every), P(every), P(every),
        P(every, None), P(every), P(every),
        P("tok", "ffn"), P("ffn", "tok"), P("ffn", "tok"),
        P(every), P(every), P(every),
    )
    return jax.shard_map(local, mesh=mesh, in_specs=placed, out_specs=given, check_vma=False)
```

profile of v0, /device:TPU:0, one launch (start us, length us, event | category | flops | bytes accessed | tf_op | source)
XLA Modules:
  0.0 281.3 jit_solution(2671740003002846869)
XLA Ops:
  7.2 1.5 convolution_convert_fusion.x_ref.xpick_ref
  8.7 2.4 add_convert_fusion.6.k_ref
  16.0 30.5 %attend_picked.1 = (bf16[80,768]{1,0:T(8,128)(2,1)S(1)}, bf16[12,80,512]{2,1,0:T(8,128)(2,1)S(1)}, f32[12,512,512]{2,1,0:T(8,128)}, s32[512,128]{1,0:T(8,128)S(1...) custom-call(s32[80]{0:T(128)S(1)} %bitcast.72, ...), custom_call_target="tpu_custom_call" | custom-call | tf_op jit(solution)/shard_map/attend_picked/pallas_call | solution.py:276
  46.5 0.9 copy-done.50
  50.7 3.0 %collective-permute-start = (bf16[80,768]{1,0:T(8,128)(2,1)}, bf16[80,768]{1,0:T(8,128)(2,1)}, u32[]{:S(2)}, u32[]{:S(2)}) collective-permute-start(bf16[80,768]{1,0:T(8,128)(2,1)} %get-tuple-element.88.mine_ref), channel_id=1, source_target_pairs={{0,1},{1,0},{2,3},{3,2},{4,5},{5,4},{6,7},{7,6},{8,9},{9,8},{10,11... | collective-permute-start | bytes 368648 | tf_op jit(solution)/shard_map/ppermute | solution.py:880
  53.8 1.1 copy-done.17
  54.9 0.9 copy-done.36
  55.8 1.1 copy-done.59
  57.0 0.9 copy-done.80
  58.6 3.7 %turn_blocks.1 = (bf16[512,768]{1,0:T(8,128)(2,1)S(1)}, bf16[80,768]{1,0:T(8,128)(2,1)S(1)}, bf16[80,768]{1,0:T(8,128)(2,1)S(1)}, bf16[512,768]{1,0:T(8,128)(2,1)S(1)}) custom-call(s32[3]{0:T(128)S(1)} %pad_add_fusion.me_ref, s32[8,768]{1,0:T(8,128)S(1)} %copy-done.100, s32[8,512]{1,0:T(8,128)S(1)} %copy-done.86, bf16[512,768]{1,0:T(8,128)(2,1)S(1)} %copy-done.17, ...), custom_call_target="tpu_custom_call" | custom-call | tf_op jit(solution)/shard_map/turn_blocks/pallas_call | solution.py:541
  62.3 1.0 copy-done.29
  64.9 3.8 %ffn_picked.1 = (bf16[80,768]{1,0:T(8,128)(2,1)S(1)}, bf16[80,768]{1,0:T(8,128)(2,1)S(1)}, bf16[160,1536]{1,0:T(8,128)(2,1)S(1)}, f32[160,1536]{1,0:T(8,128)S(1)}) custom-call(bf16[80,768]{1,0:T(8,128)(2,1)} %get-tuple-element.88.mine_ref, bf16[80,768]{1,0:T(8,128)(2,1)} %collective-permute-done.their_ref, bf16[768,1536]{1,0:T(8,128)(2,1)S(1)} %copy-done, ...), custom_call_target="tpu_custom_call" | custom-call | tf_op jit(solution)/shard_map/ffn_picked/pallas_call | solution.py:580
  68.9 1.7 add_convert_fusion.2.q_ref
  70.6 3.2 %collective-permute-done.1.got_ref = bf16[80,768]{1,0:T(8,128)(2,1)S(1)} collective-permute-done((bf16[80,768]{1,0:T(8,128)(2,1)S(1)}, bf16[80,768]{1,0:T(8,128)(2,1)S(1)}, u32[]{:S(2)}, u32[]{:S(2)}) %collective-permute-start.1) | collective-permute-done | bytes 122912 | tf_op jit(solution)/shard_map/ppermute | solution.py:880
  74.4 2.4 norm_picked.1
  78.3 3.6 %collective-permute-done.2.their_ref.dtheir_ref = bf16[80,768]{1,0:T(8,128)(2,1)} collective-permute-done((bf16[80,768]{1,0:T(8,128)(2,1)}, bf16[80,768]{1,0:T(8,128)(2,1)}, u32[]{:S(2)}, u32[]{:S(2)}) %collective-permute-start.2) | collective-permute-done | bytes 122912 | tf_op jit(solution)/shard_map/ppermute | solution.py:880
  82.0 1.2 copy-done.52
  83.2 0.9 copy-done.72
  84.1 4.7 %ffn_back.1 = (bf16[80,768]{1,0:T(8,128)(2,1)S(1)}, bf16[80,768]{1,0:T(8,128)(2,1)}, bf16[160,1536]{1,0:T(8,128)(2,1)S(1)}, f32[8,1536]{1,0:T(8,128)S(1)}) custom-call(bf16[80,768]{1,0:T(8,128)(2,1)S(1)} %copy-done.72, bf16[80,768]{1,0:T(8,128)(2,1)} %collective-permute-done.2.their_ref.dtheir_ref, bf16[768,1536]{1,0:T(8,128)(2,1)S(1)} %copy-done, ...), custom_call_target="tpu_custom_call" | custom-call | tf_op jit(solution)/shard_map/ffn_back/pallas_call | solution.py:655
  89.6 1.6 constant_dynamic-slice_fusion.2
  91.3 4.3 %ffn_grads.1 = bf16[768,3072]{1,0:T(8,128)(2,1)S(1)} custom-call(bf16[80,768]{1,0:T(8,128)(2,1)} %get-tuple-element.88.mine_ref, bf16[80,768]{1,0:T(8,128)(2,1)} %collective-permute-done.their_ref, bf16[80,768]{1,0:T(8,128)(2,1)S(1)} %copy-done.73, bf16[80,768]{1,0:T(8,128)(2,1)} %collective-permute-done.2.their_ref.dtheir_ref, ...), custom_call_target="tpu_custom_call" | custom-call | tf_op jit(solution)/shard_map/ffn_grads/pallas_call | solution.py:691
  95.6 2.1 copy-done.2
  97.8 1.8 collective-permute-start.4
  100.7 0.9 copy-done.54
  101.6 1.0 copy-done.61
  102.7 0.9 copy-done.75
  103.6 0.9 copy-done.78
  104.6 0.9 copy-done.82
  109.1 39.0 %attend_back.1 = (bf16[80,768]{1,0:T(8,128)(2,1)S(1)}, bf16[512,768]{1,0:T(8,128)(2,1)S(1)}, bf16[512,768]{1,0:T(8,128)(2,1)S(1)}, bf16[2,512,768]{2,1,0:T(8,128...) custom-call(s32[3]{0:T(128)S(1)} %copy-done.109, s32[1024,128]{1,0:T(8,128)S(1)} %copy-done.61, ...), custom_call_target="tpu_custom_call" | custom-call | tf_op jit(solution)/shard_map/attend_back/pallas_call | solution.py:468
  148.3 7.4 %weight_grads.2 = (bf16[14,128,768]{2,1,0:T(8,128)(2,1)}, f32[16,768]{1,0:T(8,128)S(1)}) custom-call(bf16[512,768]{1,0:T(8,128)(2,1)S(1)} %copy-done.30, bf16[512,768]{1,0:T(8,128)(2,1)S(1)} %copy-done.33, bf16[80,768]{1,0:T(8,128)(2,1)S(1)} %copy-done.63, bf16[80,768]{1,0:T(8,128)(2,1)S(1)} %copy-done.66, ...), custom_call_target="tpu_custom_call" | custom-call | tf_op jit(solution)/shard_map/weight_grads/pallas_call | solution.py:855
  156.5 1.3 copy-done.11
  157.7 1.1 copy-done.21
  158.9 1.1 copy-done.24
  160.0 1.1 copy-done.31
  161.1 1.1 copy-done.34
  164.9 0.9 copy-done.67
  165.8 0.9 copy-done.69
  167.4 6.5 %weight_grads.3 = (bf16[14,128,768]{2,1,0:T(8,128)(2,1)}, f32[16,768]{1,0:T(8,128)}) custom-call(bf16[512,768]{1,0:T(8,128)(2,1)S(1)} %copy-done.31, bf16[512,768]{1,0:T(8,128)(2,1)S(1)} %copy-done.34, bf16[80,768]{1,0:T(8,128)(2,1)S(1)} %copy-done.64, bf16[80,768]{1,0:T(8,128)(2,1)S(1)} %copy-done.67, ...), custom_call_target="tpu_custom_call" | custom-call | tf_op jit(solution)/shard_map/weight_grads/pallas_call | solution.py:855
  173.9 3.7 %add_convert_fusion = bf16[14,128,768]{2,1,0:T(8,128)(2,1)S(1)} fusion(bf16[14,128,768]{2,1,0:T(8,128)(2,1)} %collective-permute-done.6, bf16[14,128,768]{2,1,0:T(8,128)(2,1)} %get-tuple-element.119), kind=kLoop, calls=%fused_computation | loop fusion | flops 5505024 | bytes 8257536 | tf_op jit(solution)/shard_map/convert_element_type | solution.py:942
  177.8 1.9 collective-permute-start.7
  179.6 1.5 collective-permute-start.14
  181.2 1.2 collective-permute-done.8
  182.4 1.3 collective-permute-start.9
  183.7 13.0 %attend_full.2.ctx_ref = bf16[512,384]{1,0:T(8,128)(2,1)S(1)} custom-call(s32[512,512]{1,0:T(8,128)S(1)} %bitcast.69, bf16[512,768]{1,0:T(8,128)(2,1)S(1)} %copy-done.26, bf16[512,768]{1,0:T(8,128)(2,1)S(1)} %copy-done.4, bf16[512,768]{1,0:T(8,128)(2,1)S(1)} %copy-done.8, bf16[512,768]{1,0:T(8,128)(2,1)S(1)} %copy-done.6, ...), custom_call_target="tpu_custom_call" | custom-call | tf_op jit(solution)/shard_map/attend_full/pallas_call | solution.py:352
  196.7 12.6 %collective-permute-done.9 = f32[16,768]{1,0:T(8,128)S(1)} collective-permute-done((f32[16,768]{1,0:T(8,128)S(1)}, f32[16,768]{1,0:T(8,128)S(1)}, u32[]{:S(2)}, u32[]{:S(2)}) %collective-permute-start.9) | collective-permute-done | bytes 49184 | tf_op jit(solution)/shard_map/ppermute | solution.py:904
  209.9 1.0 slice.112
  211.2 1.8 collective-permute-start.10
  213.1 1.5 select_add_fusion.2
  215.3 1.2 copy-done.15
  216.5 1.1 copy-done.27
  217.7 12.9 %attend_full.3.ctx2_ref = bf16[512,384]{1,0:T(8,128)(2,1)S(1)} custom-call(s32[512,512]{1,0:T(8,128)S(1)} %bitcast.70, bf16[512,768]{1,0:T(8,128)(2,1)S(1)} %copy-done.27, bf16[512,768]{1,0:T(8,128)(2,1)S(1)} %copy-done.4, bf16[512,768]{1,0:T(8,128)(2,1)S(1)} %copy-done.8, bf16[512,768]{1,0:T(8,128)(2,1)S(1)} %copy-done.6, ...), custom_call_target="tpu_custom_call" | custom-call | tf_op jit(solution)/shard_map/attend_full/pallas_call | solution.py:352
  231.4 1.4 add_convert_fusion.7
  234.4 1.9 collective-permute-start.12
  237.4 1.1 copy-done.22
  238.5 1.1 copy-done.25
  239.7 1.3 copy-done.44
  242.7 0.9 copy-done.77
  243.7 3.4 %token_grads.1 = f32[512,768]{1,0:T(8,128)} custom-call(bf16[80,512]{1,0:T(8,128)(2,1)S(1)} %copy-done.60, f32[80,768]{1,0:T(8,128)S(1)} %copy-done.77, bf16[80,768]{1,0:T(8,128)(2,1)S(1)} %copy-done.47, bf16[512,768]{1,0:T(8,128)(2,1)S(1)} %copy-done.22, bf16[512,768]{1,0:T(8,128)(2,1)S(1)} %copy-done.25, bf16[768,768]{1,0:T(8,128)(2,1)S(1)} %copy-done.1, ...), custom_call_target="tpu_custom_call" | custom-call | tf_op jit(solution)/shard_map/token_grads/pallas_call | solution.py:791
  247.2 1.2 add_convert_fusion.8
  248.4 3.0 %collective-permute-start.18 = (bf16[14,8,768]{2,1,0:T(8,128)(2,1)S(1)}, bf16[14,8,768]{2,1,0:T(8,128)(2,1)S(1)}, u32[]{:S(2)}, u32[]{:S(2)}) collective-permute-start(bf16[14,8,768]{2,1,0:T(8,128)(2,1)S(1)} %slice.115), channel_id=1, source_target_pairs={{0,16},{1,17},{2,18},{3,19},{4,20},{5,21},{6,22},{7,23},{8,24},{9,... | collective-permute-start | bytes 516104 | tf_op jit(solution)/shard_map/ppermute | solution.py:904
  251.6 1.1 collective-permute-done.17.bin3_ref
  252.8 1.3 copy-done.42
  254.1 14.8 %ffn_full.1 = bf16[512,768]{1,0:T(8,128)(2,1)} custom-call(bf16[512,768]{1,0:T(8,128)(2,1)S(1)} %copy-done.19, bf16[512,384]{1,0:T(8,128)(2,1)S(1)} %copy-done.38, bf16[512,384]{1,0:T(8,128)(2,1)S(1)} %copy-done.40, bf16[768,768]{1,0:T(8,128)(2,1)S(1)} %copy-done.13, f32[768]{0:T(1024)S(1)} %copy-done.103, f32[768]{0:T(1024)S(1)} %copy-done.89, ...), custom_call_target="tpu_custom_call" | custom-call | tf_op jit(solution)/shard_map/ffn_full/pallas_call | solution.py:759
  272.3 1.8 convert_bitcast_fusion
  (279 shorter events, 33.2 us)
Async XLA Ops:
  7.2 265.1 %reduce-scatter.2.cloned.1.call-start = ((), (), s32[]{:S(2)}) async-start(), calls=%async_computation.1 | async-start | bytes 5013504 | tf_op jit(solution)/shard_map/reduce_scatter | solution.py:988
  8.7 7.2 %copy-start.35 = (bf16[80,768]{1,0:T(8,128)(2,1)}, bf16[80,768]{1,0:T(8,128)(2,1)S(1)}, u32[]{:S(2)}) copy-start(bf16[80,768]{1,0:T(8,128)(2,1)S(1)} %convolution_convert_fusion.x_ref.xpick_ref) | copy-start | bytes 368644
  15.9 30.6 %copy-start.7 = (bf16[512,768]{1,0:T(8,128)(2,1)}, bf16[512,768]{1,0:T(8,128)(2,1)S(1)}, u32[]{:S(2)}) copy-start(bf16[512,768]{1,0:T(8,128)(2,1)S(1)} %add_convert_fusion.5.v_ref) | copy-start | bytes 2359300
  16.0 37.8 %copy-start.86 = (s32[8,512]{1,0:T(8,128)S(1)}, s32[8,512]{1,0:T(8,128)}, u32[]{:S(2)}) copy-start(s32[8,512]{1,0:T(8,128)} %constant.65.clone.relorder_ref.order_ref) | copy-start | bytes 49156
  16.0 48.9 %copy-start = (bf16[768,1536]{1,0:T(8,128)(2,1)S(1)}, bf16[768,1536]{1,0:T(8,128)(2,1)}, u32[]{:S(2)}) copy-start(bf16[768,1536]{1,0:T(8,128)(2,1)} %win_ref.5) | copy-start | bytes 7077892
  50.7 14.2 %collective-permute-start = (bf16[80,768]{1,0:T(8,128)(2,1)}, bf16[80,768]{1,0:T(8,128)(2,1)}, u32[]{:S(2)}, u32[]{:S(2)}) collective-permute-start(bf16[80,768]{1,0:T(8,128)(2,1)} %get-tuple-element.88.mine_ref), channel_id=1, source_target_pairs={{0,1},{1,0},{2,3},{3,2},{4,5},{5,4},{6,7},{7,6},{8,9},{9,8},{10,11... | collective-permute-start | bytes 368648 | tf_op jit(solution)/shard_map/ppermute | solution.py:880
  53.7 10.5 %copy-start.107 = (s32[1,80]{1,0:T(1,128)S(1)}, s32[1,80]{1,0:T(1,128)}, u32[]{:S(2)}) copy-start(s32[1,80]{1,0:T(1,128)} %param.26) | copy-start | bytes 964
  53.8 14.9 %copy-start.108 = (s32[3]{0:T(128)}, s32[3]{0:T(128)S(1)}, u32[]{:S(2)}) copy-start(s32[3]{0:T(128)S(1)} %pad_add_fusion.me_ref) | copy-start | bytes 40
  58.6 6.3 %copy-start.90 = (f32[1536]{0:T(1024)S(1)}, f32[1536]{0:T(1024)}, u32[]{:S(2)}) copy-start(f32[1536]{0:T(1024)} %bin_ref.1) | copy-start | bytes 18436
  68.8 4.9 %collective-permute-start.1 = (bf16[80,768]{1,0:T(8,128)(2,1)S(1)}, bf16[80,768]{1,0:T(8,128)(2,1)S(1)}, u32[]{:S(2)}, u32[]{:S(2)}) collective-permute-start(bf16[80,768]{1,0:T(8,128)(2,1)S(1)} %get-tuple-element.91), channel_id=1, source_target_pairs={{0,1},{1,0},{2,3},{3,2},{4,5},{5,4},{6,7},{7,6},{8,9},{9,8},{10,11... | collective-permute-start | bytes 368648 | tf_op jit(solution)/shard_map/ppermute | solution.py:880
  76.8 5.2 %collective-permute-start.2 = (bf16[80,768]{1,0:T(8,128)(2,1)}, bf16[80,768]{1,0:T(8,128)(2,1)}, u32[]{:S(2)}, u32[]{:S(2)}) collective-permute-start(bf16[80,768]{1,0:T(8,128)(2,1)} %get-tuple-element.95.mine_ref.dmine_ref), channel_id=1, source_target_pairs={{0,1},{1,0},{2,3},{3,2},{4,5},{5,4},{6,7},{7,6},{8,9},{9,8},{10,11... | collective-permute-start | bytes 368648 | tf_op jit(solution)/shard_map/ppermute | solution.py:880
  84.1 5.5 %copy-start.113 = (bf16[1536,768]{1,0:T(8,128)(2,1)S(1)}, bf16[1536,768]{1,0:T(8,128)(2,1)}, u32[]{:S(2)}) copy-start(bf16[1536,768]{1,0:T(8,128)(2,1)} %down_ref.5) | copy-start | bytes 7077892
  89.4 8.3 %collective-permute-start.3 = (bf16[80,768]{1,0:T(8,128)(2,1)}, bf16[80,768]{1,0:T(8,128)(2,1)}, u32[]{:S(2)}, u32[]{:S(2)}) collective-permute-start(bf16[80,768]{1,0:T(8,128)(2,1)} %get-tuple-element.98), channel_id=1, source_target_pairs={{0,1},{1,0},{2,3},{3,2},{4,5},{5,4},{6,7},{7,6},{8,9},{9,8},{10,11... | collective-permute-start | bytes 368648 | tf_op jit(solution)/shard_map/ppermute | solution.py:880
  91.2 8.6 %copy-start.4 = (bf16[512,768]{1,0:T(8,128)(2,1)S(1)}, bf16[512,768]{1,0:T(8,128)(2,1)}, u32[]{:S(2)}) copy-start(bf16[512,768]{1,0:T(8,128)(2,1)} %copy-done.3) | copy-start | bytes 2359300
  91.2 8.6 %copy-start.6 = (bf16[512,768]{1,0:T(8,128)(2,1)S(1)}, bf16[512,768]{1,0:T(8,128)(2,1)}, u32[]{:S(2)}) copy-start(bf16[512,768]{1,0:T(8,128)(2,1)} %copy-done.5) | copy-start | bytes 2359300
  91.2 8.5 %copy-start.8 = (bf16[512,768]{1,0:T(8,128)(2,1)S(1)}, bf16[512,768]{1,0:T(8,128)(2,1)}, u32[]{:S(2)}) copy-start(bf16[512,768]{1,0:T(8,128)(2,1)} %copy-done.7) | copy-start | bytes 2359300
  97.8 50.5 %collective-permute-start.4 = (bf16[768,768]{1,0:T(8,128)(2,1)}, bf16[768,768]{1,0:T(8,128)(2,1)S(1)}, u32[]{:S(2)}, u32[]{:S(2)}) collective-permute-start(bf16[768,768]{1,0:T(8,128)(2,1)} %get-tuple-element.103), channel_id=1, source_target_pairs={{0,1},{1,0},{2,3},{3,2},{4,5},{5,4},{6,7},{7,6},{8,9},{9,8},{10,11... | collective-permute-start | bytes 3538952 | tf_op jit(solution)/shard_map/ppermute | solution.py:880
  99.6 48.6 %collective-permute-start.5 = (f32[1,768]{1,0:T(1,128)}, f32[1,768]{1,0:T(1,128)S(1)}, u32[]{:S(2)}, u32[]{:S(2)}) collective-permute-start(f32[1,768]{1,0:T(1,128)} %dynamic_slice.16), channel_id=1, source_target_pairs={{0,1},{1,0},{2,3},{3,2},{4,5},{5,4},{6,7},{7,6},{8,9},{9,8},{10,11... | collective-permute-start | bytes 9224 | tf_op jit(solution)/shard_map/ppermute | solution.py:880
  109.1 39.1 %copy-start.10 = (bf16[768,768]{1,0:T(8,128)(2,1)S(1)}, bf16[768,768]{1,0:T(8,128)(2,1)}, u32[]{:S(2)}) copy-start(bf16[768,768]{1,0:T(8,128)(2,1)} %wk_ref.5) | copy-start | bytes 3538948
  109.1 39.1 %copy-start.30 = (bf16[512,768]{1,0:T(8,128)(2,1)S(1)}, bf16[512,768]{1,0:T(8,128)(2,1)}, u32[]{:S(2)}) copy-start(bf16[512,768]{1,0:T(8,128)(2,1)} %copy-done.29) | copy-start | bytes 2359300
  109.1 39.1 %copy-start.33 = (bf16[512,768]{1,0:T(8,128)(2,1)S(1)}, bf16[512,768]{1,0:T(8,128)(2,1)}, u32[]{:S(2)}) copy-start(bf16[512,768]{1,0:T(8,128)(2,1)} %copy-done.32) | copy-start | bytes 2359300
  109.1 39.2 %copy-start.56 = (f32[8,1536]{1,0:T(8,128)S(1)}, f32[8,1536]{1,0:T(8,128)}, u32[]{:S(2)}) copy-start(f32[8,1536]{1,0:T(8,128)} %copy-done.55) | copy-start | bytes 147460
  109.1 39.2 %copy-start.63 = (bf16[80,768]{1,0:T(8,128)(2,1)S(1)}, bf16[80,768]{1,0:T(8,128)(2,1)}, u32[]{:S(2)}) copy-start(bf16[80,768]{1,0:T(8,128)(2,1)} %copy-done.62) | copy-start | bytes 368644
  109.1 39.2 %copy-start.66 = (bf16[80,768]{1,0:T(8,128)(2,1)S(1)}, bf16[80,768]{1,0:T(8,128)(2,1)}, u32[]{:S(2)}) copy-start(bf16[80,768]{1,0:T(8,128)(2,1)} %copy-done.65) | copy-start | bytes 368644
  148.2 7.6 %copy-start.20 = (bf16[512,768]{1,0:T(8,128)(2,1)}, bf16[512,768]{1,0:T(8,128)(2,1)S(1)}, u32[]{:S(2)}) copy-start(bf16[512,768]{1,0:T(8,128)(2,1)S(1)} %get-tuple-element.130.dk_ref) | copy-start | bytes 2359300
  148.2 7.6 %copy-start.23 = (bf16[512,768]{1,0:T(8,128)(2,1)}, bf16[512,768]{1,0:T(8,128)(2,1)S(1)}, u32[]{:S(2)}) copy-start(bf16[512,768]{1,0:T(8,128)(2,1)S(1)} %get-tuple-element.113.dv_ref) | copy-start | bytes 2359300
  148.2 7.6 %copy-start.45 = (bf16[80,768]{1,0:T(8,128)(2,1)}, bf16[80,768]{1,0:T(8,128)(2,1)S(1)}, u32[]{:S(2)}) copy-start(bf16[80,768]{1,0:T(8,128)(2,1)S(1)} %get-tuple-element.108.dq_ref) | copy-start | bytes 368644
  148.2 7.6 %copy-start.68 = (bf16[80,768]{1,0:T(8,128)(2,1)}, bf16[80,768]{1,0:T(8,128)(2,1)S(1)}, u32[]{:S(2)}) copy-start(bf16[80,768]{1,0:T(8,128)(2,1)S(1)} %get-tuple-element.114.dattn_ref) | copy-start | bytes 368644
  148.2 7.6 %copy-start.76 = (f32[80,768]{1,0:T(8,128)}, f32[80,768]{1,0:T(8,128)S(1)}, u32[]{:S(2)}) copy-start(f32[80,768]{1,0:T(8,128)S(1)} %get-tuple-element.129.dz1_ref) | copy-start | bytes 737284
  148.2 7.6 %copy-start.84 = (f32[8,768]{1,0:T(8,128)}, f32[8,768]{1,0:T(8,128)S(1)}, u32[]{:S(2)}) copy-start(f32[8,768]{1,0:T(8,128)S(1)} %get-tuple-element.115.early_ref) | copy-start | bytes 73732
  148.2 7.6 %copy-start.111 = (f32[1,768]{1,0:T(1,128)}, f32[1,768]{1,0:T(1,128)S(1)}, u32[]{:S(2)}) copy-start(f32[1,768]{1,0:T(1,128)S(1)} %collective-permute-done.5.bin2_ref) | copy-start | bytes 9220
  148.2 7.6 %copy-start.41 = (bf16[768,768]{1,0:T(8,128)(2,1)}, bf16[768,768]{1,0:T(8,128)(2,1)S(1)}, u32[]{:S(2)}) copy-start(bf16[768,768]{1,0:T(8,128)(2,1)S(1)} %collective-permute-done.4.win2_ref) | copy-start | bytes 3538948
  156.4 17.5 %collective-permute-start.6 = (bf16[14,128,768]{2,1,0:T(8,128)(2,1)}, bf16[14,128,768]{2,1,0:T(8,128)(2,1)}, u32[]{:S(2)}, u32[]{:S(2)}) collective-permute-start(bf16[14,128,768]{2,1,0:T(8,128)(2,1)} %get-tuple-element.117), channel_id=1, source_target_pairs={{0,2},{1,3},{2,0},{3,1},{4,6},{5,7},{6,4},{7,5},{8,10},{9,11},{10,... | collective-permute-start | bytes 8257544 | tf_op jit(solution)/shard_map/ppermute | solution.py:904
  177.6 6.0 %copy-start.14 = (s32[1,512,512]{2,1,0:T(8,128)S(1)}, s32[1,512,512]{2,1,0:T(8,128)}, u32[]{:S(2)}) copy-start(s32[1,512,512]{2,1,0:T(8,128)} %param.25) | copy-start | bytes 3145732
  177.6 6.0 %copy-start.26 = (bf16[512,768]{1,0:T(8,128)(2,1)S(1)}, bf16[512,768]{1,0:T(8,128)(2,1)}, u32[]{:S(2)}) copy-start(bf16[512,768]{1,0:T(8,128)(2,1)} %add_convert_fusion.2.q_ref) | copy-start | bytes 2359300
  177.8 31.5 %collective-permute-start.7 = (bf16[14,64,768]{2,1,0:T(8,128)(2,1)S(1)}, bf16[14,64,768]{2,1,0:T(8,128)(2,1)S(1)}, u32[]{:S(2)}, u32[]{:S(2)}) collective-permute-start(bf16[14,64,768]{2,1,0:T(8,128)(2,1)S(1)} %slice.110), channel_id=1, source_target_pairs={{0,4},{1,5},{2,10},{3,11},{4,0},{5,1},{6,14},{7,15},{8,12},{9,13},... | collective-permute-start | bytes 4128776 | tf_op jit(solution)/shard_map/ppermute | solution.py:904
  179.6 35.1 %collective-permute-start.14 = (bf16[768,768]{1,0:T(8,128)(2,1)}, bf16[768,768]{1,0:T(8,128)(2,1)}, u32[]{:S(2)}, u32[]{:S(2)}) collective-permute-start(bf16[768,768]{1,0:T(8,128)(2,1)} %get-tuple-element.134), channel_id=1, source_target_pairs={{0,1},{1,0},{2,3},{3,2},{4,5},{5,4},{6,7},{7,6},{8,9},{9,8},{10,11... | collective-permute-start | bytes 3538952 | tf_op jit(solution)/shard_map/ppermute | solution.py:880
  181.1 1.2 collective-permute-start.8
  182.4 14.3 %copy-start.118 = (f32[16,768]{1,0:T(8,128)}, f32[16,768]{1,0:T(8,128)S(1)}, u32[]{:S(2)}) copy-start(f32[16,768]{1,0:T(8,128)S(1)} %add.113) | copy-start | bytes 147460
  182.4 26.9 %collective-permute-start.9 = (f32[16,768]{1,0:T(8,128)S(1)}, f32[16,768]{1,0:T(8,128)S(1)}, u32[]{:S(2)}, u32[]{:S(2)}) collective-permute-start(f32[16,768]{1,0:T(8,128)S(1)} %add.113), channel_id=1, source_target_pairs={{0,4},{1,5},{2,10},{3,11},{4,0},{5,1},{6,14},{7,15},{8,12},{9,13},... | collective-permute-start | bytes 147464 | tf_op jit(solution)/shard_map/ppermute | solution.py:904
  196.7 13.0 %copy-start.37 = (bf16[512,384]{1,0:T(8,128)(2,1)}, bf16[512,384]{1,0:T(8,128)(2,1)S(1)}, u32[]{:S(2)}) copy-start(bf16[512,384]{1,0:T(8,128)(2,1)S(1)} %attend_full.2.ctx_ref) | copy-start | bytes 1179652
  211.2 20.2 %collective-permute-start.10 = (bf16[14,32,768]{2,1,0:T(8,128)(2,1)}, bf16[14,32,768]{2,1,0:T(8,128)(2,1)}, u32[]{:S(2)}, u32[]{:S(2)}) collective-permute-start(bf16[14,32,768]{2,1,0:T(8,128)(2,1)} %slice.112), channel_id=1, source_target_pairs={{0,1},{1,0},{2,6},{3,7},{4,5},{5,4},{6,2},{7,3},{8,9},{9,8},{10,14... | collective-permute-start | bytes 2064392 | tf_op jit(solution)/shard_map/ppermute | solution.py:904
  214.6 16.9 %collective-permute-start.11 = (f32[16,768]{1,0:T(8,128)}, f32[16,768]{1,0:T(8,128)}, u32[]{:S(2)}, u32[]{:S(2)}) collective-permute-start(f32[16,768]{1,0:T(8,128)} %select_add_fusion.2), channel_id=1, source_target_pairs={{0,1},{1,0},{2,6},{3,7},{4,5},{5,4},{6,2},{7,3},{8,9},{9,8},{10,14... | collective-permute-start | bytes 147464 | tf_op jit(solution)/shard_map/ppermute | solution.py:904
  214.8 37.9 %collective-permute-start.15 = (bf16[768,768]{1,0:T(8,128)(2,1)}, bf16[768,768]{1,0:T(8,128)(2,1)}, u32[]{:S(2)}, u32[]{:S(2)}) collective-permute-start(bf16[768,768]{1,0:T(8,128)(2,1)} %copy-done.41), channel_id=1, source_target_pairs={{0,2},{2,0},{4,6},{6,4},{8,10},{10,8},{12,14},{14,12},{16,18},{18,... | collective-permute-start | bytes 3538952 | tf_op jit(solution)/shard_map/ppermute | solution.py:880
  214.8 37.9 %collective-permute-start.16 = (bf16[768,768]{1,0:T(8,128)(2,1)}, bf16[768,768]{1,0:T(8,128)(2,1)}, u32[]{:S(2)}, u32[]{:S(2)}) collective-permute-start(bf16[768,768]{1,0:T(8,128)(2,1)} %collective-permute-done.14.down2_ref), channel_id=1, source_target_pairs={{0,2},{2,0},{4,6},{6,4},{8,10},{10,8},{12,14},{14,12},{16,18},{18,... | collective-permute-start | bytes 3538952 | tf_op jit(solution)/shard_map/ppermute | solution.py:880
  217.7 13.8 %copy-start.115 = (bf16[14,64,768]{2,1,0:T(8,128)(2,1)S(1)}, bf16[14,64,768]{2,1,0:T(8,128)(2,1)}, u32[]{:S(2)}) copy-start(bf16[14,64,768]{2,1,0:T(8,128)(2,1)} %copy-done.114) | copy-start | bytes 4128772
  231.4 6.0 %copy-start.12 = (bf16[768,768]{1,0:T(8,128)(2,1)S(1)}, bf16[768,768]{1,0:T(8,128)(2,1)}, u32[]{:S(2)}) copy-start(bf16[768,768]{1,0:T(8,128)(2,1)} %wk_ref.5) | copy-start | bytes 3538948
  234.4 12.7 %collective-permute-start.12 = (bf16[14,16,768]{2,1,0:T(8,128)(2,1)}, bf16[14,16,768]{2,1,0:T(8,128)(2,1)}, u32[]{:S(2)}, u32[]{:S(2)}) collective-permute-start(bf16[14,16,768]{2,1,0:T(8,128)(2,1)} %slice.114), channel_id=1, source_target_pairs={{0,8},{1,9},{2,3},{3,2},{4,12},{5,13},{6,7},{7,6},{8,0},{9,1},{10,... | collective-permute-start | bytes 1032200 | tf_op jit(solution)/shard_map/ppermute | solution.py:904
  237.2 9.9 %collective-permute-start.13 = (f32[16,768]{1,0:T(8,128)S(1)}, f32[16,768]{1,0:T(8,128)S(1)}, u32[]{:S(2)}, u32[]{:S(2)}) collective-permute-start(f32[16,768]{1,0:T(8,128)S(1)} %select_add_fusion.1), channel_id=1, source_target_pairs={{0,8},{1,9},{2,3},{3,2},{4,12},{5,13},{6,7},{7,6},{8,0},{9,1},{10,... | collective-permute-start | bytes 147464 | tf_op jit(solution)/shard_map/ppermute | solution.py:904
  243.7 7.8 %copy-start.112 = (f32[1,768]{1,0:T(1,128)S(1)}, f32[1,768]{1,0:T(1,128)}, u32[]{:S(2)}) copy-start(f32[1,768]{1,0:T(1,128)} %copy-done.111) | copy-start | bytes 9220
  243.7 7.9 %copy-start.91 = (f32[1536]{0:T(1024)S(1)}, f32[1536]{0:T(1024)}, u32[]{:S(2)}) copy-start(f32[1536]{0:T(1024)} %bin_ref.1) | copy-start | bytes 18436
  243.7 9.0 %copy-start.19 = (bf16[512,768]{1,0:T(8,128)(2,1)S(1)}, bf16[512,768]{1,0:T(8,128)(2,1)}, u32[]{:S(2)}) copy-start(bf16[512,768]{1,0:T(8,128)(2,1)} %x_ref.2) | copy-start | bytes 2359300
  243.7 9.0 %copy-start.40 = (bf16[512,384]{1,0:T(8,128)(2,1)S(1)}, bf16[512,384]{1,0:T(8,128)(2,1)}, u32[]{:S(2)}) copy-start(bf16[512,384]{1,0:T(8,128)(2,1)} %copy-done.39) | copy-start | bytes 1179652
  243.7 9.0 %copy-start.110 = (f32[768]{0:T(1024)S(1)}, f32[768]{0:T(1024)}, u32[]{:S(2)}) copy-start(f32[768]{0:T(1024)} %bias2_ref.1) | copy-start | bytes 9220
  247.1 5.6 %copy-start.13 = (bf16[768,768]{1,0:T(8,128)(2,1)S(1)}, bf16[768,768]{1,0:T(8,128)(2,1)}, u32[]{:S(2)}) copy-start(bf16[768,768]{1,0:T(8,128)(2,1)} %wo_ref.5) | copy-start | bytes 3538948
  247.1 5.6 %copy-start.38 = (bf16[512,384]{1,0:T(8,128)(2,1)S(1)}, bf16[512,384]{1,0:T(8,128)(2,1)}, u32[]{:S(2)}) copy-start(bf16[512,384]{1,0:T(8,128)(2,1)} %copy-done.37) | copy-start | bytes 1179652
  247.1 5.6 %copy-start.89 = (f32[768]{0:T(1024)S(1)}, f32[768]{0:T(1024)}, u32[]{:S(2)}) copy-start(f32[768]{0:T(1024)} %gain1_ref.3) | copy-start | bytes 9220
  247.1 5.6 %copy-start.99 = (f32[768]{0:T(1024)S(1)}, f32[768]{0:T(1024)}, u32[]{:S(2)}) copy-start(f32[768]{0:T(1024)} %bias1_ref.3) | copy-start | bytes 9220
  247.1 5.6 %copy-start.103 = (f32[768]{0:T(1024)S(1)}, f32[768]{0:T(1024)}, u32[]{:S(2)}) copy-start(f32[768]{0:T(1024)} %bo_ref.3) | copy-start | bytes 9220
  247.1 5.6 %copy-start.104 = (f32[768]{0:T(1024)S(1)}, f32[768]{0:T(1024)}, u32[]{:S(2)}) copy-start(f32[768]{0:T(1024)} %bdown_ref.3) | copy-start | bytes 9220
  247.1 5.6 %copy-start.105 = (f32[768]{0:T(1024)S(1)}, f32[768]{0:T(1024)}, u32[]{:S(2)}) copy-start(f32[768]{0:T(1024)} %gain2_ref.3) | copy-start | bytes 9220
  248.4 20.5 %collective-permute-start.18 = (bf16[14,8,768]{2,1,0:T(8,128)(2,1)S(1)}, bf16[14,8,768]{2,1,0:T(8,128)(2,1)S(1)}, u32[]{:S(2)}, u32[]{:S(2)}) collective-permute-start(bf16[14,8,768]{2,1,0:T(8,128)(2,1)S(1)} %slice.115), channel_id=1, source_target_pairs={{0,16},{1,17},{2,18},{3,19},{4,20},{5,21},{6,22},{7,23},{8,24},{9,... | collective-permute-start | bytes 516104 | tf_op jit(solution)/shard_map/ppermute | solution.py:904
  251.4 17.4 %collective-permute-start.19 = (f32[16,768]{1,0:T(8,128)S(1)}, f32[16,768]{1,0:T(8,128)}, u32[]{:S(2)}, u32[]{:S(2)}) collective-permute-start(f32[16,768]{1,0:T(8,128)S(1)} %select_add_fusion), channel_id=1, source_target_pairs={{0,16},{1,17},{2,18},{3,19},{4,20},{5,21},{6,22},{7,23},{8,24},{9,... | collective-permute-start | bytes 147464 | tf_op jit(solution)/shard_map/ppermute | solution.py:904
  251.5 1.2 collective-permute-start.17
  (82 other events, 115.5 us)
Sparse Core Ops, SparseCore 0:
  156.6 83.9 reduce-scatter.1
where the time goes:
time: 287 us; the launch traced here: 281 us
  Pallas kernels  146 us (51%)
  local copies, waits for them, and re-layouts  57.7 us (20%)
  waiting for transfers between devices  21.7 us (8%)
  starting transfers between devices  17.9 us (6%)
  between operations  15.4 us (5%)
  other arithmetic  13.9 us (5%)
  matrix products  8.21 us (3%)
    unnamed x252, local copies, waits for them, and re-layouts  51.6 us
    pallas_call x1, Pallas kernels, attend_back(): pl.pallas_call(back_kernel, grid=(pairs,), in_specs=[pl.BlockSpec(memory_...  39 us
    pallas_call x1, Pallas kernels, attend_picked(): pl.pallas_call(picked_kernel, grid=(pairs,), in_specs=[pl.BlockSpec(memor...  30.5 us
    pallas_call x2, Pallas kernels, attend_full(): pl.pallas_call(full_kernel, grid=(pairs,), in_specs=[pl.BlockSpec((seq, s...  26 us
    pallas_call x1, Pallas kernels, ffn_full(): pl.pallas_call(ffn_full_kernel, grid=(8,), in_specs=[whole(value) for val...  14.8 us
    pallas_call x2, Pallas kernels, weight_grads(): pl.pallas_call(functools.partial(grads_kernel, half), grid=(width // grou...  13.9 us
    ppermute x10, waiting for transfers between devices, send(): return lax.ppermute(values, self.axes, pairs)  13.8 us
    ppermute x10, starting transfers between devices, send(): return lax.ppermute(values, self.axes, pairs)  10.3 us
  transfers between devices with their start and end apart: 21, of which 5 were waited for; matrix products, arithmetic and copies ran while one was open for 7% of the time, Pallas kernels for 35%

commit v1 on v0

--- a/solution.py
+++ b/solution.py
@@ -17,6 +17,7 @@
 norm_eps = 1e-07
 bf16 = jnp.bfloat16
 f32 = jnp.float32
+PARAMS = pltpu.CompilerParams(vmem_limit_bytes=60 * 2**20)
 
 
 def dot_nn(first_op, second_op):
@@ -303,7 +304,7 @@
             pltpu.VMEM((picks, width), f32),
             pltpu.SMEM((seq // HALF * (seq // LANES),), jnp.int32),
         ],
-        compiler_params=pltpu.CompilerParams(vmem_limit_bytes=48 * 2**20),
+        compiler_params=PARAMS,
         name="attend_picked",
     )(
         positions, rel_ids, q_pick, k, v, pos_key, pos_query, x_pick, w_out, b_out, gain, bias
@@ -365,7 +366,7 @@
             pltpu.VMEM((2, seq, seq), bf16),
             pltpu.SMEM((seq // HALF * (seq // LANES),), jnp.int32),
         ],
-        compiler_params=pltpu.CompilerParams(vmem_limit_bytes=48 * 2**20),
+        compiler_params=PARAMS,
         name="attend_full",
     )(rel_ids, q, k, v, pos_key, key_scores)
 
@@ -499,7 +500,7 @@
             pltpu.VMEM((2 * seq, table), bf16),
             pltpu.SMEM((seq // LANES,), jnp.int32),
         ],
-        compiler_params=pltpu.CompilerParams(vmem_limit_bytes=48 * 2**20),
+        compiler_params=PARAMS,
         name="attend_back",
     )(
         me, table_of, order, words, words_pick, q_pick, k, v, probs, pos_key, pos_query,
@@ -546,7 +547,7 @@
         out_specs=[col(value) for value in given],
         out_shape=[jax.ShapeDtypeStruct(value.shape, bf16) for value in given],
         scratch_shapes=[pltpu.VMEM(rel_table.shape, bf16)],
-        compiler_params=pltpu.CompilerParams(vmem_limit_bytes=48 * 2**20),
+        compiler_params=PARAMS,
         name="turn_blocks",
     )(me, order, rel_order, *given)
 
@@ -592,7 +593,7 @@
             jax.ShapeDtypeStruct((2 * picks, hidden_cols), f32),
         ],
         scratch_shapes=[pltpu.VMEM((2 * picks, width), f32)],
-        compiler_params=pltpu.CompilerParams(vmem_limit_bytes=48 * 2**20),
+        compiler_params=PARAMS,
         name="ffn_picked",
     )(mine, theirs, w_in, b_in, w_down)
 
@@ -624,6 +625,7 @@
             jax.ShapeDtypeStruct((picks, width), bf16),
             jax.ShapeDtypeStruct((8, width), f32),
         ],
+        compiler_params=PARAMS,
         name="norm_picked",
     )(normed, gain1, bias1, mine, got, b_down, gain2, grads, pick)
 
@@ -666,41 +668,57 @@
             jax.ShapeDtypeStruct((8, hidden_cols), f32),
         ],
         scratch_shapes=[pltpu.VMEM((2 * picks, width), f32)],
-        compiler_params=pltpu.CompilerParams(vmem_limit_bytes=48 * 2**20),
+        compiler_params=PARAMS,
         name="ffn_back",
     )(mine, theirs, w_in, w_down, slope)
 
 
-def ffn_grads_kernel(mine_ref, their_ref, dmine_ref, dtheir_ref, dpre_ref, hidden_ref, out_ref):
-    @pl.when(pl.program_id(0) == 0)
-    def _():
-        rows = jnp.concatenate([mine_ref[...], their_ref[...]], axis=0)
-        out_ref[...] = dot_tn(rows, dpre_ref[...]).astype(bf16)
-
-    @pl.when(pl.program_id(0) == 1)
-    def _():
-        rows = jnp.concatenate([dmine_ref[...], dtheir_ref[...]], axis=0)
-        out_ref[...] = dot_tn(rows, hidden_ref[...]).astype(bf16)
-
-
-def ffn_grads(mine, theirs, dmine, dtheirs, dpre, hidden):
+def ffn_grads_kernel(
+    half, me_ref, order_ref, mine_ref, their_ref, dmine_ref, dtheir_ref, dpre_ref, hidden_ref,
+    out_ref, left,
+):
+    first = pl.program_id(0) == 0
+
+    @pl.when(pl.program_id(1) == 0)
+    def _():
+        width = mine_ref.shape[1]
+        cols = slice(half * (width // 2), (half + 1) * (width // 2))
+        source = block_source(order_ref, me_ref, cols, width)
+        spot = lax.broadcasted_iota(jnp.int32, (width, width // 2), 0)
+        chosen = (spot == source).astype(f32).astype(bf16)
+        mine = jnp.where(first, mine_ref[...], dmine_ref[...])
+        theirs = jnp.where(first, their_ref[...], dtheir_ref[...])
+        left[...] = dot_nn(jnp.concatenate([mine, theirs], axis=0), chosen).astype(bf16)
+
+    @pl.when(first)
+    def _():
+        out_ref[...] = dot_tn(left[...], dpre_ref[...]).astype(bf16)
+
+    @pl.when(jnp.logical_not(first))
+    def _():
+        out_ref[...] = dot_tn(left[...], hidden_ref[...]).astype(bf16)
+
+
+def ffn_grads(half, me, order, mine, theirs, dmine, dtheirs, dpre, hidden):
     picks, width = mine.shape
     hidden_cols = dpre.shape[1]
     tile = hidden_cols // 3
-    whole = pl.BlockSpec((picks, width), lambda n, t: (0, 0))
+    whole = lambda value: pl.BlockSpec(value.shape, lambda n, t: (0, 0))
     return pl.pallas_call(
-        ffn_grads_kernel,
+        functools.partial(ffn_grads_kernel, half),
         grid=(2, 3),
         in_specs=[
-            whole, whole, whole, whole,
+            pl.BlockSpec(memory_space=pltpu.SMEM),
+            whole(order), whole(mine), whole(mine), whole(mine), whole(mine),
             pl.BlockSpec((2 * picks, tile), lambda n, t: (0, jnp.where(n == 0, t, 2))),
             pl.BlockSpec((2 * picks, tile), lambda n, t: (0, jnp.where(n == 0, 0, t))),
         ],
-        out_specs=pl.BlockSpec((width, tile), lambda n, t: (0, 3 * n + t)),
-        out_shape=jax.ShapeDtypeStruct((width, 2 * hidden_cols), bf16),
-        compiler_params=pltpu.CompilerParams(vmem_limit_bytes=48 * 2**20),
+        out_specs=pl.BlockSpec((width // 2, tile), lambda n, t: (0, 3 * n + t)),
+        out_shape=jax.ShapeDtypeStruct((width // 2, 2 * hidden_cols), bf16),
+        scratch_shapes=[pltpu.VMEM((2 * picks, width // 2), bf16)],
+        compiler_params=PARAMS,
         name="ffn_grads",
-    )(mine, theirs, dmine, dtheirs, dpre, hidden)
+    )(me, order, mine, theirs, dmine, dtheirs, dpre, hidden)
 
 
 def ffn_full_kernel(
@@ -765,7 +783,7 @@
         scratch_shapes=[
             pltpu.VMEM((rows, width), f32), pltpu.VMEM((rows, width), bf16), pltpu.VMEM((rows, width), f32)
         ],
-        compiler_params=pltpu.CompilerParams(vmem_limit_bytes=48 * 2**20),
+        compiler_params=PARAMS,
         name="ffn_full",
     )(*head, *[value for shard in shards for value in shard], *tail)
 
@@ -794,7 +812,7 @@
         in_specs=[whole(pick), col(dz1.shape[0]), whole(dq), whole(dk), whole(dv), row, row, row],
         out_specs=col(seq),
         out_shape=jax.ShapeDtypeStruct((seq, width), f32),
-        compiler_params=pltpu.CompilerParams(vmem_limit_bytes=48 * 2**20),
+        compiler_params=PARAMS,
         name="token_grads",
     )(pick, dz1, dq, dk, dv, w_query, w_key, w_value)
 
@@ -868,7 +886,7 @@
             jax.ShapeDtypeStruct((planes, LANES, width), bf16),
             jax.ShapeDtypeStruct((16, width), f32),
         ],
-        compiler_params=pltpu.CompilerParams(vmem_limit_bytes=48 * 2**20),
+        compiler_params=PARAMS,
         name="weight_grads",
     )(
         x, rel, x_pick, c_pick, dpos, dq, dk, dv, dattn, dpos, dpos, w_query, w_key, early, bins, bins
@@ -946,7 +964,10 @@
     over_all = Halving(("tok", "ffn"), n_ffn, [2 * n_ffn, 1, 4 * n_ffn], n_all)
     own, own_rel = width // n_all, table_rows // n_all
     unit = math.gcd(own, own_rel)
+    over_tok = Halving("tok", 1, [2, 4], n_tok)
     me = jnp.stack([over_all.me, over_all.upper, jnp.int32(n_all)])
+    me_tok = jnp.stack([over_tok.me, over_tok.upper, jnp.int32(n_tok)])
+    tok_order = over_tok.order(width, width // n_tok)
     order, rel_order = over_all.order(width, unit), over_all.order(table_rows, unit)
     table_of = jnp.asarray(np.repeat(distance_rows(seq, table_rows)[:, None], LANES, 1))
 
@@ -983,17 +1004,37 @@
     dffn_theirs = swap(dffn, "ffn", 1)
     dpart, dtheirs, dpre, gb_in = ffn_back(dffn, dffn_theirs, w_in, w_down, slope)
     dgot = swap(dtheirs, "ffn", 1)
-    gw_ffn = ffn_grads(h1_mine, h1_theirs, dffn, dffn_theirs, after(dpre, dtheirs), hidden)
-    dgot = after(dgot, gw_ffn)
-    s_ffn = lax.psum_scatter(gw_ffn, "tok", scatter_dimension=0, tiled=True)
-
-    in_half, bias_half, down_half = after((in_half, bias_half, down_half), dgot)
+    def halves(values, axis):
+        size = values.shape[axis] // 2
+        cut = lambda at: lax.slice_in_dim(values, at, at + size, axis=axis)
+        return cut(0), cut(size)
+
+    add = lambda one, other: low(wide(one) + wide(other))
+
+    def next_halves(kept, got, axis):
+        pieces = [add(one, other) for one, other in zip(halves(kept, axis), halves(got, axis))]
+        return pieces
+
+    def ffn_half(half, dpre):
+        return ffn_grads(
+            half, me_tok, tok_order, h1_mine, h1_theirs, dffn, dffn_theirs, dpre, hidden
+        )
+
+    ffn_sent = ffn_half(1, after(dpre, dtheirs))
+    ffn_got = over_tok.send(ffn_sent, 0)
+    in_half, bias_half, down_half = after((in_half, bias_half, down_half), ffn_sent)
+    ffn_kept = ffn_half(0, after(dpre, ffn_sent))
+    dgot = after(dgot, ffn_kept)
     far_in, far_bias = swap(in_half, "ffn", 1), swap(bias_half, "ffn", 1)
+    ffn_kept, ffn_sent = next_halves(ffn_kept, ffn_got, 0)
+    ffn_got = over_tok.send(ffn_sent, 1)
     dq, dk, dv, dpos, dz1, dattn, early = attend_back(
         me, table_of, rel_order, words, words_pick, q_pick, k, v, probs, pos_query, pos_key,
-        dz2, dpart, after(dgot, in_half), normed1, inv1, ln1_gain, w_out, early,
-    )
-    far_in, far_bias = after((far_in, far_bias), dk)
+        dz2, dpart, after(dgot, in_half, ffn_sent), normed1, inv1, ln1_gain, w_out, early,
+    )
+    far_in, far_bias, ffn_got = after((far_in, far_bias, ffn_got), dk)
+    ffn_kept, ffn_sent = next_halves(ffn_kept, ffn_got, 0)
+    ffn_got = over_tok.send(ffn_sent, 2)
 
     def grads(half, dk):
         return weight_grads(
@@ -1001,21 +1042,16 @@
             w_query, w_key, early, gb_in,
         )
 
-    all_send, vectors = grads(1, after(dk, far_in))
+    all_send, vectors = grads(1, after(dk, far_in, ffn_sent))
     near_in, near_bias = swap(far_in, "tok", 1), swap(far_bias, "tok", 1)
     far_down = swap(after(down_half, far_in), "ffn", 1)
 
-    def halves(values, axis):
-        size = values.shape[axis] // 2
-        cut = lambda at: lax.slice_in_dim(values, at, at + size, axis=axis)
-        return cut(0), cut(size)
-
-    add = lambda one, other: low(wide(one) + wide(other))
     all_got = over_all.send(all_send, 0)
     vec_got = over_all.send(vectors, 0)
     all_kept, _ = grads(0, after(dk, all_send))
-    all_sums = add(all_kept, after(all_got, all_kept))
+    all_kept, all_sent = next_halves(all_kept, after(all_got, all_kept), 1)
     vectors = vectors + vec_got
+    ffn_step = 3
     shared = lax.broadcasted_iota(jnp.int32, (vectors.shape[0], 1), 0) < 9
 
     def attend(first, count, q):
@@ -1023,16 +1059,15 @@
 
     fills = []
     for step in range(1, over_all.steps):
-        kept, sent = halves(all_sums, 1)
-        all_got = over_all.send(sent, step)
+        all_got = over_all.send(all_sent, step)
         vec_got = over_all.send(vectors, step)
         if step == 1:
-            fills.append(attend(0, pairs // 2, after(q, sent)))
+            fills.append(attend(0, pairs // 2, after(q, all_sent)))
         elif step == 2:
-            fills.append(attend(pairs // 2, pairs - pairs // 2, after(q, sent)))
+            fills.append(attend(pairs // 2, pairs - pairs // 2, after(q, all_sent)))
         elif step == 3:
             fills.append(
-                token_grads(pick, dz1, dq, after(dk, sent), dv, w_query, w_key, w_value)
+                token_grads(pick, dz1, dq, after(dk, all_sent), dv, w_query, w_key, w_value)
             )
         elif step == 4:
             near_down = swap(far_down, "tok", 1)
@@ -1041,15 +1076,34 @@
             ]
             fills.append(
                 ffn_full(
-                    after(tokens, sent), fills[:2], w_out, b_out, ln1_gain, ln1_bias, shards,
+                    after(tokens, all_sent), fills[:2], w_out, b_out, ln1_gain, ln1_bias, shards,
                     b_down, ln2_gain, ln2_bias,
                 )
             )
         if step <= 4:
             all_got, vec_got = after((all_got, vec_got), fills[-1])
-        all_sums = add(kept, all_got)
+        if step <= 2 and ffn_step <= over_tok.steps:
+            ffn_got = after(ffn_got, fills[-1])
+            if ffn_step < over_tok.steps:
+                ffn_kept, ffn_sent = next_halves(ffn_kept, ffn_got, 0)
+                ffn_got = over_tok.send(ffn_sent, ffn_step)
+                all_got = after(all_got, ffn_sent)
+            else:
+                ffn_kept = add(ffn_kept, ffn_got)
+            ffn_step += 1
+        if step < over_all.steps - 1:
+            all_kept, all_sent = next_halves(all_kept, all_got, 1)
+        else:
+            all_sums = add(all_kept, all_got)
         vectors = vectors + jnp.where(shared | (over_all.bit(step) != 1), vec_got, 0.0)
     grad_tokens, output = fills[2:]
+    for step in range(ffn_step, over_tok.steps + 1):
+        if step < over_tok.steps:
+            ffn_kept, ffn_sent = next_halves(ffn_kept, ffn_got, 0)
+            ffn_got = over_tok.send(ffn_sent, step)
+        else:
+            ffn_kept = add(ffn_kept, ffn_got)
+    s_ffn = ffn_kept
 
     all_sums = all_sums.reshape(all_sums.shape[0] * unit, width)
     s_w = [wide(all_sums[n * own : (n + 1) * own]) for n in range(4)]

time: 287 us -> 269 us (0.937)
  local copies, waits for them, and re-layouts: 57.7 us -> 10.1 us
  Pallas kernels: 146 us -> 167 us
  between operations: 15.4 us -> 1.22 us
  waiting for transfers between devices: 21.7 us -> 31.1 us
  other arithmetic: 13.9 us -> 20.5 us
  matrix products: 8.21 us -> 12.5 us
  starting transfers between devices: 17.9 us -> 21.9 us
    unnamed x252 -> x56, local copies, waits for them, and re-layouts: 51.6 us -> 5.11 us
    ppermute x10, waiting for transfers between devices: 7.94 us -> 24.3 us  [swap(): return lax.ppermute(values, axis, [(n, n ^ bit) for n in range(size)])]
    pallas_call x1 -> x2, Pallas kernels: 4.34 us -> 12.5 us  [ffn_grads(): pl.pallas_call(functools.partial(ffn_grads_kernel, half), grid=(2, 3), in...]
    convert_element_type x6 -> x10, other arithmetic: 7.34 us -> 15.3 us  [local(): low = lambda value: value.astype(bf16)]
    ppermute x10 -> x14, waiting for transfers between devices: 13.8 us -> 6.82 us  [send(): return lax.ppermute(values, self.axes, pairs)]
    ppermute x10 -> x14, starting transfers between devices: 10.3 us -> 15.2 us  [send(): return lax.ppermute(values, self.axes, pairs)]
    dot_general x7, matrix products: 8.21 us -> 12.5 us  [dot_nn(): lax.dot_general(first_op, second_op, (((1,), (0,)), ((), ())), preferred_...]
  transfers between devices with their start and end apart: 21 -> 24, of which waited for: 5 -> 6; matrix products, arithmetic and copies ran while one was open for 7% -> 7% of each run, Pallas kernels for 35% -> 41%
where the time goes in v1:
time: 269 us; the launch traced here: 265 us
  Pallas kernels  167 us (62%)
  waiting for transfers between devices  31.1 us (12%)
  starting transfers between devices  21.9 us (8%)
  other arithmetic  20.5 us (8%)
  matrix products  12.5 us (5%)
  local copies, waits for them, and re-layouts  10.1 us (4%)
    pallas_call x1, Pallas kernels, attend_back(): pl.pallas_call(back_kernel, grid=(pairs,), in_specs=[pl.BlockSpec(memory_...  39.1 us
    pallas_call x1, Pallas kernels, attend_picked(): pl.pallas_call(picked_kernel, grid=(pairs,), in_specs=[pl.BlockSpec(memor...  30.5 us
    pallas_call x2, Pallas kernels, attend_full(): pl.pallas_call(full_kernel, grid=(pairs,), in_specs=[pl.BlockSpec((seq, s...  28 us
    ppermute x10, waiting for transfers between devices, swap(): return lax.ppermute(values, axis, [(n, n ^ bit) for n in range(size)])  24.3 us
    pallas_call x1, Pallas kernels, ffn_full(): pl.pallas_call(ffn_full_kernel, grid=(8,), in_specs=[whole(value) for val...  16.3 us
    pallas_call x2, Pallas kernels, weight_grads(): pl.pallas_call(functools.partial(grads_kernel, half), grid=(width // grou...  16.2 us
    convert_element_type x10, other arithmetic, local(): low = lambda value: value.astype(bf16)  15.3 us
    ppermute x14, starting transfers between devices, send(): return lax.ppermute(values, self.axes, pairs)  15.2 us
  transfers between devices with their start and end apart: 24, of which 6 were waited for; matrix products, arithmetic and copies ran while one was open for 7% of the time, Pallas kernels for 41%

profile of v1, /device:TPU:0, one launch (start us, length us, event | category | flops | bytes accessed | tf_op | source)
XLA Modules:
  0.0 264.8 jit_solution(5758663809544616106)
XLA Ops:
  0.7 1.5 convolution_convert_fusion.x_ref.xpick_ref
  2.2 3.3 %add_convert_fusion.8.k_ref = bf16[512,768]{1,0:T(8,128)(2,1)} fusion(bf16[512,768]{1,0:T(8,128)(2,1)} %x_ref.2, bf16[768,768]{1,0:T(8,128)(2,1)} %wk_ref.5, f32[768]{0:T(1024)} %param.34), kind=kOutput, calls=%fused_computation.8 | convolution fusion | flops 604766208 | bytes 2755584 | tf_op jit(solution)/shard_map/dot_general | solution.py:24
  5.5 1.7 add_convert_fusion.6.pk_ref
  7.2 1.7 add_convert_fusion.5.pq_ref
  8.9 1.0 fusion.qc_ref
  10.0 1.7 add_convert_fusion.7.v_ref
  11.7 30.5 %attend_picked.1 = (bf16[80,768]{1,0:T(8,128)(2,1)}, bf16[12,80,512]{2,1,0:T(8,128)(2,1)}, f32[12,512,512]{2,1,0:T(8,128)}, s32[512,128]{1,0:T(8,128)}, s32[80,1...) custom-call(s32[80]{0:T(128)} %bitcast.77, s32[512,512]{1,0:T(8,128)} %bitcast.70, ...), custom_call_target="tpu_custom_call" | custom-call | tf_op jit(solution)/shard_map/attend_picked/pallas_call | solution.py:277
  42.2 3.0 %collective-permute-start = (bf16[80,768]{1,0:T(8,128)(2,1)}, bf16[80,768]{1,0:T(8,128)(2,1)S(1)}, u32[]{:S(2)}, u32[]{:S(2)}) collective-permute-start(bf16[80,768]{1,0:T(8,128)(2,1)} %get-tuple-element.93.mine_ref), channel_id=1, source_target_pairs={{0,1},{1,0},{2,3},{3,2},{4,5},{5,4},{6,7},{7,6},{8,9},{9,8},{10,11... | collective-permute-start | bytes 368648 | tf_op jit(solution)/shard_map/ppermute | solution.py:898
  45.3 0.6 pad_add_fusion.me_ref
  45.9 5.4 %turn_blocks.1 = (bf16[512,768]{1,0:T(8,128)(2,1)}, bf16[80,768]{1,0:T(8,128)(2,1)}, bf16[80,768]{1,0:T(8,128)(2,1)}, bf16[512,768]{1,0:T(8,128)(2,1)}) custom-call(s32[3]{0:T(128)} %pad_add_fusion.me_ref, s32[8,768]{1,0:T(8,128)} %constant.81.clone.order_ref, s32[8,512]{1,0:T(8,128)} %constant.82.clone.relorder_ref.order_ref, bf16[512,768]{1,0:T(8,128)(2,1)} %x_ref.2, ...), custom_call_target="tpu_custom_call" | custom-call | tf_op jit(solution)/shard_map/turn_blocks/pallas_call | solution.py:542
  51.2 0.7 fusion.1.pick_ref
  52.0 0.7 copy-done.10
  52.6 5.3 %ffn_picked.1 = (bf16[80,768]{1,0:T(8,128)(2,1)}, bf16[80,768]{1,0:T(8,128)(2,1)}, bf16[160,1536]{1,0:T(8,128)(2,1)}, f32[160,1536]{1,0:T(8,128)}) custom-call(bf16[80,768]{1,0:T(8,128)(2,1)} %get-tuple-element.93.mine_ref, bf16[80,768]{1,0:T(8,128)(2,1)} %copy-done.10, bf16[768,1536]{1,0:T(8,128)(2,1)} %win_ref.5, f32[1536]{0:T(1024)} %bin_ref.1, ...), custom_call_target="tpu_custom_call" | custom-call | tf_op jit(solution)/shard_map/ffn_picked/pallas_call | solution.py:581
  57.9 1.7 add_convert_fusion.4.q_ref
  59.6 3.4 %collective-permute-done.1.got_ref = bf16[80,768]{1,0:T(8,128)(2,1)S(1)} collective-permute-done((bf16[80,768]{1,0:T(8,128)(2,1)}, bf16[80,768]{1,0:T(8,128)(2,1)S(1)}, u32[]{:S(2)}, u32[]{:S(2)}) %collective-permute-start.1) | collective-permute-done | bytes 122912 | tf_op jit(solution)/shard_map/ppermute | solution.py:898
  63.0 0.6 copy-done.17
  63.6 2.4 norm_picked.1
  66.3 0.6 pad_add_fusion.1.me_ref
  66.9 4.3 %collective-permute-done.2.their_ref.dtheir_ref = bf16[80,768]{1,0:T(8,128)(2,1)S(1)} collective-permute-done((bf16[80,768]{1,0:T(8,128)(2,1)}, bf16[80,768]{1,0:T(8,128)(2,1)S(1)}, u32[]{:S(2)}, u32[]{:S(2)}) %collective-permute-start.2) | collective-permute-done | bytes 122912 | tf_op jit(solution)/shard_map/ppermute | solution.py:898
  71.1 0.6 copy-done.11
  71.8 5.8 %ffn_back.1 = (bf16[80,768]{1,0:T(8,128)(2,1)}, bf16[80,768]{1,0:T(8,128)(2,1)}, bf16[160,1536]{1,0:T(8,128)(2,1)}, f32[8,1536]{1,0:T(8,128)}) custom-call(bf16[80,768]{1,0:T(8,128)(2,1)} %get-tuple-element.100.mine_ref.dmine_ref, bf16[80,768]{1,0:T(8,128)(2,1)} %copy-done.11, bf16[768,1536]{1,0:T(8,128)(2,1)} %win_ref.5, bf16[1536,768]{1,0:T(8,128)(2,1)} %down_ref.5, ...), custom_call_target="tpu_custom_call" | custom-call | tf_op jit(solution)/shard_map/ffn_back/pallas_call | solution.py:657
  77.6 6.3 %ffn_grads.2 = bf16[384,3072]{1,0:T(8,128)(2,1)} custom-call(s32[3]{0:T(128)} %pad_add_fusion.1.me_ref, s32[8,768]{1,0:T(8,128)} %constant.80.clone.order_ref, bf16[80,768]{1,0:T(8,128)(2,1)} %get-tuple-element.93.mine_ref, bf16[80,768]{1,0:T(8,128)(2,1)} %copy-done.10, bf16[80,768]{1,0:T(8,128)(2,1)} %get-tuple-element.100.mine_ref.dmine_ref, ...), custom_call_target="tpu_custom_call" | custom-call | tf_op jit(solution)/shard_map/ffn_grads/pallas_call | solution.py:707
  84.0 2.5 constant_dynamic-slice_fusion.2
  86.7 6.1 %ffn_grads.3 = bf16[384,3072]{1,0:T(8,128)(2,1)} custom-call(s32[3]{0:T(128)} %pad_add_fusion.1.me_ref, s32[8,768]{1,0:T(8,128)} %constant.80.clone.order_ref, bf16[80,768]{1,0:T(8,128)(2,1)} %get-tuple-element.93.mine_ref, bf16[80,768]{1,0:T(8,128)(2,1)} %copy-done.10, bf16[80,768]{1,0:T(8,128)(2,1)} %get-tuple-element.100.mine_ref.dmine_ref, ...), custom_call_target="tpu_custom_call" | custom-call | tf_op jit(solution)/shard_map/ffn_grads/pallas_call | solution.py:707
  92.9 4.3 %add_convert_fusion.2 = (bf16[192,3072]{1,0:T(8,128)(2,1)S(1)}, bf16[192,3072]{1,0:T(8,128)(2,1)}) fusion(bf16[384,3072]{1,0:T(8,128)(2,1)} %collective-permute-done.4, bf16[384,3072]{1,0:T(8,128)(2,1)} %ffn_grads.3), kind=kLoop, calls=%fused_computation.2 | loop fusion | flops 4718592 | bytes 7077888 | tf_op jit(solution)/shard_map/convert_element_type | solution.py:960
  97.2 1.8 collective-permute-start.7
  98.9 1.5 collective-permute-start.3
  100.9 16.6 %collective-permute-done.3.got_ref = bf16[80,768]{1,0:T(8,128)(2,1)S(1)} collective-permute-done((bf16[80,768]{1,0:T(8,128)(2,1)S(1)}, bf16[80,768]{1,0:T(8,128)(2,1)S(1)}, u32[]{:S(2)}, u32[]{:S(2)}) %collective-permute-start.3) | collective-permute-done | bytes 122912 | tf_op jit(solution)/shard_map/ppermute | solution.py:898
  117.6 0.7 copy-done.16
  118.2 39.1 %attend_back.1 = (bf16[80,768]{1,0:T(8,128)(2,1)}, bf16[512,768]{1,0:T(8,128)(2,1)}, bf16[512,768]{1,0:T(8,128)(2,1)}, bf16[2,512,768]{2,1,0:T(8,128)(2,1)}, f32...) custom-call(s32[3]{0:T(128)} %pad_add_fusion.me_ref, s32[1024,128]{1,0:T(8,128)} %constant.83.clone.row_ref, ...), custom_call_target="tpu_custom_call" | custom-call | tf_op jit(solution)/shard_map/attend_back/pallas_call | solution.py:469
  157.4 3.1 %add_convert_fusion.11 = (bf16[96,3072]{1,0:T(8,128)(2,1)}, bf16[96,3072]{1,0:T(8,128)(2,1)}) fusion(bf16[192,3072]{1,0:T(8,128)(2,1)S(1)} %get-tuple-element.151, bf16[192,3072]{1,0:T(8,128)(2,1)} %collective-permute-done.7), kind=kLoop, calls=%fused_computation.11 | loop fusion | flops 2359296 | bytes 3538944 | tf_op jit(solution)/shard_map/convert_element_type | solution.py:960
  160.5 8.1 %weight_grads.2 = (bf16[14,128,768]{2,1,0:T(8,128)(2,1)}, f32[16,768]{1,0:T(8,128)}) custom-call(bf16[512,768]{1,0:T(8,128)(2,1)} %get-tuple-element.85.x_ref, bf16[512,768]{1,0:T(8,128)(2,1)} %get-tuple-element.86.rel_ref, bf16[80,768]{1,0:T(8,128)(2,1)} %get-tuple-element.87.xpick_ref, bf16[80,768]{1,0:T(8,128)(2,1)} %get-tuple-element.88.cpick_ref, ...), custom_call_target="tpu_custom_call" | custom-call | tf_op jit(solution)/shard_map/weight_grads/pallas_call | solution.py:873
  168.7 8.1 %weight_grads.3 = (bf16[14,128,768]{2,1,0:T(8,128)(2,1)}, f32[16,768]{1,0:T(8,128)}) custom-call(bf16[512,768]{1,0:T(8,128)(2,1)} %get-tuple-element.85.x_ref, bf16[512,768]{1,0:T(8,128)(2,1)} %get-tuple-element.86.rel_ref, bf16[80,768]{1,0:T(8,128)(2,1)} %get-tuple-element.87.xpick_ref, bf16[80,768]{1,0:T(8,128)(2,1)} %get-tuple-element.88.cpick_ref, ...), custom_call_target="tpu_custom_call" | custom-call | tf_op jit(solution)/shard_map/weight_grads/pallas_call | solution.py:873
  176.8 3.9 %add_convert_fusion = (bf16[14,64,768]{2,1,0:T(8,128)(2,1)}, bf16[14,64,768]{2,1,0:T(8,128)(2,1)S(1)}) fusion(bf16[14,128,768]{2,1,0:T(8,128)(2,1)S(1)} %collective-permute-done.8, bf16[14,128,768]{2,1,0:T(8,128)(2,1)} %get-tuple-element.126), kind=kLoop, calls=%fused_computation | loop fusion | flops 5505024 | bytes 8257536 | tf_op jit(solution)/shard_map/convert_element_type | solution.py:960
  180.7 1.5 collective-permute-start.9
  182.2 1.6 collective-permute-start.12
  184.3 0.7 collective-permute-done.10
  185.0 0.6 collective-permute-start.11
  185.6 14.1 %attend_full.2.ctx_ref = bf16[512,384]{1,0:T(8,128)(2,1)} custom-call(s32[512,512]{1,0:T(8,128)} %bitcast.71, bf16[512,768]{1,0:T(8,128)(2,1)} %add_convert_fusion.4.q_ref, bf16[512,768]{1,0:T(8,128)(2,1)} %add_convert_fusion.8.k_ref, bf16[512,768]{1,0:T(8,128)(2,1)} %add_convert_fusion.7.v_ref, bf16[512,768]{1,0:T(8,128)(2,1)} %add_convert_fusion.6.pk_ref, ...), custom_call_target="tpu_custom_call" | custom-call | tf_op jit(solution)/shard_map/attend_full/pallas_call | solution.py:353
  199.7 0.9 add_convert_fusion.17
  200.6 5.5 %collective-permute-done.11 = f32[16,768]{1,0:T(8,128)S(1)} collective-permute-done((f32[16,768]{1,0:T(8,128)S(1)}, f32[16,768]{1,0:T(8,128)S(1)}, u32[]{:S(2)}, u32[]{:S(2)}) %collective-permute-start.11) | collective-permute-done | bytes 49184 | tf_op jit(solution)/shard_map/ppermute | solution.py:922
  206.1 0.6 copy-done.20
  206.7 1.3 add_convert_fusion.9
  208.3 2.9 %collective-permute-start.23 = (bf16[48,3072]{1,0:T(8,128)(2,1)}, bf16[48,3072]{1,0:T(8,128)(2,1)S(1)}, u32[]{:S(2)}, u32[]{:S(2)}) collective-permute-start(bf16[48,3072]{1,0:T(8,128)(2,1)} %add_convert_fusion.17), channel_id=1, source_target_pairs={{0,16},{2,18},{4,20},{6,22},{8,24},{10,26},{12,28},{14,30},{16,0},... | collective-permute-start | bytes 884744 | tf_op jit(solution)/shard_map/ppermute | solution.py:922
  211.2 0.9 select_add_fusion.2
  212.1 1.5 collective-permute-start.14
  213.6 1.3 reshape.79.bin_ref
  214.9 13.9 %attend_full.3.ctx2_ref = bf16[512,384]{1,0:T(8,128)(2,1)} custom-call(s32[512,512]{1,0:T(8,128)} %bitcast.72, bf16[512,768]{1,0:T(8,128)(2,1)} %add_convert_fusion.4.q_ref, bf16[512,768]{1,0:T(8,128)(2,1)} %add_convert_fusion.8.k_ref, bf16[512,768]{1,0:T(8,128)(2,1)} %add_convert_fusion.7.v_ref, bf16[512,768]{1,0:T(8,128)(2,1)} %add_convert_fusion.6.pk_ref, ...), custom_call_target="tpu_custom_call" | custom-call | tf_op jit(solution)/shard_map/attend_full/pallas_call | solution.py:353
  228.8 0.6 collective-permute-start.20
  229.5 0.6 copy-done.19
  230.1 0.9 select_add_fusion.1
  231.0 1.3 collective-permute-start.16
  232.2 0.9 add_convert_fusion.13
  233.1 0.8 collective-permute-start.15
  234.0 5.9 %token_grads.1 = f32[512,768]{1,0:T(8,128)} custom-call(bf16[80,512]{1,0:T(8,128)(2,1)} %fusion.1.pick_ref, f32[80,768]{1,0:T(8,128)} %get-tuple-element.138.dz1_ref, bf16[80,768]{1,0:T(8,128)(2,1)} %get-tuple-element.114.dq_ref, bf16[512,768]{1,0:T(8,128)(2,1)} %get-tuple-element.139.dk_ref, bf16[512,768]{1,0:T(8,128)(2,1)} %get-tuple-element.120.dv_ref, ...), custom_call_target="tpu_custom_call" | custom-call | tf_op jit(solution)/shard_map/token_grads/pallas_call | solution.py:809
  240.0 0.6 collective-permute-done.15
  241.0 2.7 %collective-permute-start.21 = (bf16[14,8,768]{2,1,0:T(8,128)(2,1)S(1)}, bf16[14,8,768]{2,1,0:T(8,128)(2,1)S(1)}, u32[]{:S(2)}, u32[]{:S(2)}) collective-permute-start(bf16[14,8,768]{2,1,0:T(8,128)(2,1)S(1)} %add_convert_fusion.20), channel_id=1, source_target_pairs={{0,16},{1,17},{2,18},{3,19},{4,20},{5,21},{6,22},{7,23},{8,24},{9,... | collective-permute-start | bytes 516104 | tf_op jit(solution)/shard_map/ppermute | solution.py:922
  243.7 0.9 convert_bitcast_fusion
  244.6 1.0 copy-done.8
  245.6 16.3 %ffn_full.1 = bf16[512,768]{1,0:T(8,128)(2,1)} custom-call(bf16[512,768]{1,0:T(8,128)(2,1)} %x_ref.2, bf16[512,384]{1,0:T(8,128)(2,1)} %attend_full.2.ctx_ref, bf16[512,384]{1,0:T(8,128)(2,1)} %attend_full.3.ctx2_ref, bf16[768,768]{1,0:T(8,128)(2,1)} %wo_ref.5, f32[768]{0:T(1024)} %bo_ref.3, f32[768]{0:T(1024)} %gain1_ref.3, f32[768]{0:T(1024)} %bias1_ref.3, ...), custom_call_target="tpu_custom_call" | custom-call | tf_op jit(solution)/shard_map/ffn_full/pallas_call | solution.py:777
  262.0 0.7 fusion.3
  262.7 0.6 fusion.7
  263.3 0.6 constant_dynamic-slice_fusion.1
  263.9 0.6 dynamic-slice_bitcast_fusion
  (90 shorter events, 3.0 us)
Async XLA Ops:
  2.1 6.7 %copy-start.6 = (bf16[80,768]{1,0:T(8,128)(2,1)}, bf16[80,768]{1,0:T(8,128)(2,1)S(1)}, u32[]{:S(2)}) copy-start(bf16[80,768]{1,0:T(8,128)(2,1)S(1)} %convolution_convert_fusion.x_ref.xpick_ref) | copy-start | bytes 368644
  2.1 3.3 %copy-start.2 = (bf16[768,768]{1,0:T(8,128)(2,1)S(1)}, bf16[768,768]{1,0:T(8,128)(2,1)}, u32[]{:S(2)}) copy-start(bf16[768,768]{1,0:T(8,128)(2,1)} %wk_ref.5) | copy-start | bytes 3538948
  2.1 3.3 %copy-start.12 = (bf16[512,768]{1,0:T(8,128)(2,1)S(1)}, bf16[512,768]{1,0:T(8,128)(2,1)}, u32[]{:S(2)}) copy-start(bf16[512,768]{1,0:T(8,128)(2,1)} %rel_ref.1) | copy-start | bytes 2359300
  2.1 3.3 %copy-start.25 = (f32[768]{0:T(1024)S(1)}, f32[768]{0:T(1024)}, u32[]{:S(2)}) copy-start(f32[768]{0:T(1024)} %param.34) | copy-start | bytes 9220
  5.5 1.7 copy-start.1
  5.5 1.7 copy-start.23
  7.2 2.7 %copy-start.9 = (bf16[768,768]{1,0:T(8,128)(2,1)S(1)}, bf16[768,768]{1,0:T(8,128)(2,1)}, u32[]{:S(2)}) copy-start(bf16[768,768]{1,0:T(8,128)(2,1)} %wv_ref.1) | copy-start | bytes 3538948
  8.9 1.1 copy-start.3
  8.9 1.1 copy-start.26
  42.2 9.0 %copy-start.22 = (s32[1,80]{1,0:T(1,128)S(1)}, s32[1,80]{1,0:T(1,128)}, u32[]{:S(2)}) copy-start(s32[1,80]{1,0:T(1,128)} %param.27) | copy-start | bytes 964
  42.2 9.7 %collective-permute-start = (bf16[80,768]{1,0:T(8,128)(2,1)}, bf16[80,768]{1,0:T(8,128)(2,1)S(1)}, u32[]{:S(2)}, u32[]{:S(2)}) collective-permute-start(bf16[80,768]{1,0:T(8,128)(2,1)} %get-tuple-element.93.mine_ref), channel_id=1, source_target_pairs={{0,1},{1,0},{2,3},{3,2},{4,5},{5,4},{6,7},{7,6},{8,9},{9,8},{10,11... | collective-permute-start | bytes 368648 | tf_op jit(solution)/shard_map/ppermute | solution.py:898
  52.0 0.7 copy-start.10
  52.6 5.3 %copy-start.4 = (bf16[512,768]{1,0:T(8,128)(2,1)S(1)}, bf16[512,768]{1,0:T(8,128)(2,1)}, u32[]{:S(2)}) copy-start(bf16[512,768]{1,0:T(8,128)(2,1)} %x_ref.2) | copy-start | bytes 2359300
  57.9 5.1 %collective-permute-start.1 = (bf16[80,768]{1,0:T(8,128)(2,1)}, bf16[80,768]{1,0:T(8,128)(2,1)S(1)}, u32[]{:S(2)}, u32[]{:S(2)}) collective-permute-start(bf16[80,768]{1,0:T(8,128)(2,1)} %get-tuple-element.96), channel_id=1, source_target_pairs={{0,1},{1,0},{2,3},{3,2},{4,5},{5,4},{6,7},{7,6},{8,9},{9,8},{10,11... | collective-permute-start | bytes 368648 | tf_op jit(solution)/shard_map/ppermute | solution.py:898
  63.0 0.7 copy-start.17
  66.1 5.1 %collective-permute-start.2 = (bf16[80,768]{1,0:T(8,128)(2,1)}, bf16[80,768]{1,0:T(8,128)(2,1)S(1)}, u32[]{:S(2)}, u32[]{:S(2)}) collective-permute-start(bf16[80,768]{1,0:T(8,128)(2,1)} %get-tuple-element.100.mine_ref.dmine_ref), channel_id=1, source_target_pairs={{0,1},{1,0},{2,3},{3,2},{4,5},{5,4},{6,7},{7,6},{8,9},{9,8},{10,11... | collective-permute-start | bytes 368648 | tf_op jit(solution)/shard_map/ppermute | solution.py:898
  71.1 0.7 copy-start.11
  77.6 6.4 %copy-start.18 = (f32[1536]{0:T(1024)S(1)}, f32[1536]{0:T(1024)}, u32[]{:S(2)}) copy-start(f32[1536]{0:T(1024)} %bin_ref.1) | copy-start | bytes 18436
  77.6 6.4 %copy-start = (bf16[768,1536]{1,0:T(8,128)(2,1)S(1)}, bf16[768,1536]{1,0:T(8,128)(2,1)}, u32[]{:S(2)}) copy-start(bf16[768,1536]{1,0:T(8,128)(2,1)} %win_ref.5) | copy-start | bytes 7077892
  83.9 8.9 %collective-permute-start.4 = (bf16[384,3072]{1,0:T(8,128)(2,1)}, bf16[384,3072]{1,0:T(8,128)(2,1)}, u32[]{:S(2)}, u32[]{:S(2)}) collective-permute-start(bf16[384,3072]{1,0:T(8,128)(2,1)} %ffn_grads.2), channel_id=1, source_target_pairs={{0,2},{2,0},{4,6},{6,4},{8,10},{10,8},{12,14},{14,12},{16,18},{18,... | collective-permute-start | bytes 7077896 | tf_op jit(solution)/shard_map/ppermute | solution.py:922
  86.5 70.9 %collective-permute-start.5 = (bf16[768,768]{1,0:T(8,128)(2,1)S(1)}, bf16[768,768]{1,0:T(8,128)(2,1)S(1)}, u32[]{:S(2)}, u32[]{:S(2)}) collective-permute-start(bf16[768,768]{1,0:T(8,128)(2,1)S(1)} %get-tuple-element.109), channel_id=1, source_target_pairs={{0,1},{1,0},{2,3},{3,2},{4,5},{5,4},{6,7},{7,6},{8,9},{9,8},{10,11... | collective-permute-start | bytes 3538952 | tf_op jit(solution)/shard_map/ppermute | solution.py:898
  92.8 6.1 %copy-start.24 = (bf16[80,768]{1,0:T(8,128)(2,1)S(1)}, bf16[80,768]{1,0:T(8,128)(2,1)}, u32[]{:S(2)}) copy-start(bf16[80,768]{1,0:T(8,128)(2,1)} %get-tuple-element.103) | copy-start | bytes 368644
  97.2 60.2 %collective-permute-start.7 = (bf16[192,3072]{1,0:T(8,128)(2,1)}, bf16[192,3072]{1,0:T(8,128)(2,1)}, u32[]{:S(2)}, u32[]{:S(2)}) collective-permute-start(bf16[192,3072]{1,0:T(8,128)(2,1)} %get-tuple-element.152), channel_id=1, source_target_pairs={{0,4},{2,10},{4,0},{6,14},{8,12},{10,2},{12,8},{14,6},{16,20},{18,... | collective-permute-start | bytes 3538952 | tf_op jit(solution)/shard_map/ppermute | solution.py:922
  98.9 18.7 %collective-permute-start.3 = (bf16[80,768]{1,0:T(8,128)(2,1)S(1)}, bf16[80,768]{1,0:T(8,128)(2,1)S(1)}, u32[]{:S(2)}, u32[]{:S(2)}) collective-permute-start(bf16[80,768]{1,0:T(8,128)(2,1)S(1)} %copy-done.24), channel_id=1, source_target_pairs={{0,1},{1,0},{2,3},{3,2},{4,5},{5,4},{6,7},{7,6},{8,9},{9,8},{10,11... | collective-permute-start | bytes 368648 | tf_op jit(solution)/shard_map/ppermute | solution.py:898
  100.5 56.9 %collective-permute-start.6 = (f32[1,768]{1,0:T(1,128)S(1)}, f32[1,768]{1,0:T(1,128)}, u32[]{:S(2)}, u32[]{:S(2)}) collective-permute-start(f32[1,768]{1,0:T(1,128)S(1)} %dynamic_slice.16), channel_id=1, source_target_pairs={{0,1},{1,0},{2,3},{3,2},{4,5},{5,4},{6,7},{7,6},{8,9},{9,8},{10,11... | collective-permute-start | bytes 9224 | tf_op jit(solution)/shard_map/ppermute | solution.py:898
  117.6 0.7 copy-start.16
  157.4 11.2 %copy-start.7 = (bf16[768,768]{1,0:T(8,128)(2,1)}, bf16[768,768]{1,0:T(8,128)(2,1)S(1)}, u32[]{:S(2)}) copy-start(bf16[768,768]{1,0:T(8,128)(2,1)S(1)} %collective-permute-done.5.win2_ref) | copy-start | bytes 3538948
  168.6 8.2 %collective-permute-start.8 = (bf16[14,128,768]{2,1,0:T(8,128)(2,1)}, bf16[14,128,768]{2,1,0:T(8,128)(2,1)S(1)}, u32[]{:S(2)}, u32[]{:S(2)}) collective-permute-start(bf16[14,128,768]{2,1,0:T(8,128)(2,1)} %get-tuple-element.124), channel_id=1, source_target_pairs={{0,2},{1,3},{2,0},{3,1},{4,6},{5,7},{6,4},{7,5},{8,10},{9,11},{10,... | collective-permute-start | bytes 8257544 | tf_op jit(solution)/shard_map/ppermute | solution.py:922
  176.8 6.9 %copy-start.21 = (f32[16,768]{1,0:T(8,128)S(1)}, f32[16,768]{1,0:T(8,128)}, u32[]{:S(2)}) copy-start(f32[16,768]{1,0:T(8,128)} %get-tuple-element.128) | copy-start | bytes 147460
  180.7 25.4 %collective-permute-start.9 = (bf16[14,64,768]{2,1,0:T(8,128)(2,1)}, bf16[14,64,768]{2,1,0:T(8,128)(2,1)S(1)}, u32[]{:S(2)}, u32[]{:S(2)}) collective-permute-start(bf16[14,64,768]{2,1,0:T(8,128)(2,1)} %get-tuple-element.149), channel_id=1, source_target_pairs={{0,4},{1,5},{2,10},{3,11},{4,0},{5,1},{6,14},{7,15},{8,12},{9,13},... | collective-permute-start | bytes 4128776 | tf_op jit(solution)/shard_map/ppermute | solution.py:922
  182.2 17.5 %collective-permute-start.12 = (bf16[96,3072]{1,0:T(8,128)(2,1)}, bf16[96,3072]{1,0:T(8,128)(2,1)S(1)}, u32[]{:S(2)}, u32[]{:S(2)}) collective-permute-start(bf16[96,3072]{1,0:T(8,128)(2,1)} %get-tuple-element.156), channel_id=1, source_target_pairs={{0,8},{2,6},{4,12},{6,2},{8,0},{10,14},{12,4},{14,10},{16,24},{18,... | collective-permute-start | bytes 1769480 | tf_op jit(solution)/shard_map/ppermute | solution.py:922
  183.8 1.2 collective-permute-start.10
  183.8 45.0 %collective-permute-start.17 = (bf16[768,768]{1,0:T(8,128)(2,1)}, bf16[768,768]{1,0:T(8,128)(2,1)}, u32[]{:S(2)}, u32[]{:S(2)}) collective-permute-start(bf16[768,768]{1,0:T(8,128)(2,1)} %get-tuple-element.143), channel_id=1, source_target_pairs={{0,1},{1,0},{2,3},{3,2},{4,5},{5,4},{6,7},{7,6},{8,9},{9,8},{10,11... | collective-permute-start | bytes 3538952 | tf_op jit(solution)/shard_map/ppermute | solution.py:898
  185.0 14.7 %copy-start.15 = (f32[16,768]{1,0:T(8,128)}, f32[16,768]{1,0:T(8,128)S(1)}, u32[]{:S(2)}) copy-start(f32[16,768]{1,0:T(8,128)S(1)} %add.150) | copy-start | bytes 147460
  185.0 21.1 %collective-permute-start.11 = (f32[16,768]{1,0:T(8,128)S(1)}, f32[16,768]{1,0:T(8,128)S(1)}, u32[]{:S(2)}, u32[]{:S(2)}) collective-permute-start(f32[16,768]{1,0:T(8,128)S(1)} %add.150), channel_id=1, source_target_pairs={{0,4},{1,5},{2,10},{3,11},{4,0},{5,1},{6,14},{7,15},{8,12},{9,13},... | collective-permute-start | bytes 147464 | tf_op jit(solution)/shard_map/ppermute | solution.py:922
  185.6 14.1 %copy-start.5 = (bf16[96,3072]{1,0:T(8,128)(2,1)S(1)}, bf16[96,3072]{1,0:T(8,128)(2,1)}, u32[]{:S(2)}) copy-start(bf16[96,3072]{1,0:T(8,128)(2,1)} %get-tuple-element.155) | copy-start | bytes 1769476
  199.7 6.4 %copy-start.13 = (bf16[96,3072]{1,0:T(8,128)(2,1)}, bf16[96,3072]{1,0:T(8,128)(2,1)S(1)}, u32[]{:S(2)}) copy-start(bf16[96,3072]{1,0:T(8,128)(2,1)S(1)} %collective-permute-done.12) | copy-start | bytes 1769476
  206.1 0.6 copy-start.20
  208.0 22.1 %collective-permute-start.13 = (bf16[14,32,768]{2,1,0:T(8,128)(2,1)}, bf16[14,32,768]{2,1,0:T(8,128)(2,1)S(1)}, u32[]{:S(2)}, u32[]{:S(2)}) collective-permute-start(bf16[14,32,768]{2,1,0:T(8,128)(2,1)} %get-tuple-element.153), channel_id=1, source_target_pairs={{0,1},{1,0},{2,6},{3,7},{4,5},{5,4},{6,2},{7,3},{8,9},{9,8},{10,14... | collective-permute-start | bytes 2064392 | tf_op jit(solution)/shard_map/ppermute | solution.py:922
  208.3 21.1 %collective-permute-start.23 = (bf16[48,3072]{1,0:T(8,128)(2,1)}, bf16[48,3072]{1,0:T(8,128)(2,1)S(1)}, u32[]{:S(2)}, u32[]{:S(2)}) collective-permute-start(bf16[48,3072]{1,0:T(8,128)(2,1)} %add_convert_fusion.17), channel_id=1, source_target_pairs={{0,16},{2,18},{4,20},{6,22},{8,24},{10,26},{12,28},{14,30},{16,0},... | collective-permute-start | bytes 884744 | tf_op jit(solution)/shard_map/ppermute | solution.py:922
  212.1 17.4 %collective-permute-start.14 = (f32[16,768]{1,0:T(8,128)S(1)}, f32[16,768]{1,0:T(8,128)S(1)}, u32[]{:S(2)}, u32[]{:S(2)}) collective-permute-start(f32[16,768]{1,0:T(8,128)S(1)} %select_add_fusion.2), channel_id=1, source_target_pairs={{0,1},{1,0},{2,6},{3,7},{4,5},{5,4},{6,2},{7,3},{8,9},{9,8},{10,14... | collective-permute-start | bytes 147464 | tf_op jit(solution)/shard_map/ppermute | solution.py:922
  214.9 29.7 %collective-permute-start.18 = (bf16[768,768]{1,0:T(8,128)(2,1)}, bf16[768,768]{1,0:T(8,128)(2,1)S(1)}, u32[]{:S(2)}, u32[]{:S(2)}) collective-permute-start(bf16[768,768]{1,0:T(8,128)(2,1)} %copy-done.7), channel_id=1, source_target_pairs={{0,2},{2,0},{4,6},{6,4},{8,10},{10,8},{12,14},{14,12},{16,18},{18,... | collective-permute-start | bytes 3538952 | tf_op jit(solution)/shard_map/ppermute | solution.py:898
  228.8 5.1 %copy-start.14 = (bf16[96,3072]{1,0:T(8,128)(2,1)S(1)}, bf16[96,3072]{1,0:T(8,128)(2,1)}, u32[]{:S(2)}) copy-start(bf16[96,3072]{1,0:T(8,128)(2,1)} %copy-done.13) | copy-start | bytes 1769476
  228.8 15.8 %collective-permute-start.20 = (f32[1,768]{1,0:T(1,128)}, f32[1,768]{1,0:T(1,128)}, u32[]{:S(2)}, u32[]{:S(2)}) collective-permute-start(f32[1,768]{1,0:T(1,128)} %collective-permute-done.6.bin2_ref), channel_id=1, source_target_pairs={{0,2},{2,0},{4,6},{6,4},{8,10},{10,8},{12,14},{14,12},{16,18},{18,... | collective-permute-start | bytes 9224 | tf_op jit(solution)/shard_map/ppermute | solution.py:898
  229.4 15.2 %collective-permute-start.19 = (bf16[768,768]{1,0:T(8,128)(2,1)}, bf16[768,768]{1,0:T(8,128)(2,1)}, u32[]{:S(2)}, u32[]{:S(2)}) collective-permute-start(bf16[768,768]{1,0:T(8,128)(2,1)} %collective-permute-done.17.down2_ref), channel_id=1, source_target_pairs={{0,2},{2,0},{4,6},{6,4},{8,10},{10,8},{12,14},{14,12},{16,18},{18,... | collective-permute-start | bytes 3538952 | tf_op jit(solution)/shard_map/ppermute | solution.py:898
  229.5 0.6 copy-start.19
  231.0 9.0 %collective-permute-start.16 = (f32[16,768]{1,0:T(8,128)S(1)}, f32[16,768]{1,0:T(8,128)S(1)}, u32[]{:S(2)}, u32[]{:S(2)}) collective-permute-start(f32[16,768]{1,0:T(8,128)S(1)} %select_add_fusion.1), channel_id=1, source_target_pairs={{0,8},{1,9},{2,3},{3,2},{4,12},{5,13},{6,7},{7,6},{8,0},{9,1},{10,... | collective-permute-start | bytes 147464 | tf_op jit(solution)/shard_map/ppermute | solution.py:922
  233.1 7.5 %collective-permute-start.15 = (bf16[14,16,768]{2,1,0:T(8,128)(2,1)}, bf16[14,16,768]{2,1,0:T(8,128)(2,1)S(1)}, u32[]{:S(2)}, u32[]{:S(2)}) collective-permute-start(bf16[14,16,768]{2,1,0:T(8,128)(2,1)} %get-tuple-element.157), channel_id=1, source_target_pairs={{0,8},{1,9},{2,3},{3,2},{4,12},{5,13},{6,7},{7,6},{8,0},{9,1},{10,... | collective-permute-start | bytes 1032200 | tf_op jit(solution)/shard_map/ppermute | solution.py:922
  240.7 21.2 %collective-permute-start.22 = (f32[16,768]{1,0:T(8,128)S(1)}, f32[16,768]{1,0:T(8,128)S(1)}, u32[]{:S(2)}, u32[]{:S(2)}) collective-permute-start(f32[16,768]{1,0:T(8,128)S(1)} %select_add_fusion), channel_id=1, source_target_pairs={{0,16},{1,17},{2,18},{3,19},{4,20},{5,21},{6,22},{7,23},{8,24},{9,... | collective-permute-start | bytes 147464 | tf_op jit(solution)/shard_map/ppermute | solution.py:922
  241.0 20.8 %collective-permute-start.21 = (bf16[14,8,768]{2,1,0:T(8,128)(2,1)S(1)}, bf16[14,8,768]{2,1,0:T(8,128)(2,1)S(1)}, u32[]{:S(2)}, u32[]{:S(2)}) collective-permute-start(bf16[14,8,768]{2,1,0:T(8,128)(2,1)S(1)} %add_convert_fusion.20), channel_id=1, source_target_pairs={{0,16},{1,17},{2,18},{3,19},{4,20},{5,21},{6,22},{7,23},{8,24},{9,... | collective-permute-start | bytes 516104 | tf_op jit(solution)/shard_map/ppermute | solution.py:922
  244.6 1.0 copy-start.8
